TPU v7x, 32 devices: a whole 2x2x4 slice. The times are simulated.
32 devices in a mesh: owner: 16 (over z, x, core), dense: 2 (over y).
Axes of the slice: x: 2, y: 2, z: 4, core: 2. Of those that a mesh axis runs over, the one named last changes fastest.
Arguments:
- owners: int32 [8192, 13, 4], P(('owner', 'dense')), may hold values from 0 to 15, all different within a row; in each aligned block of 3328 rows (0 to 3327, 3328 to 6655, ..., all dimensions but the last counted through in order) at most 1664 rows name the same one
- local_rows: int32 [8192, 13, 4], P(('owner', 'dense')), may hold values from 0 to 2047, as said below
- weights: float32 [8192, 13, 4], P(('owner', 'dense')), may hold values from 0.25 to 4
- labels: bfloat16 [8192], P(('owner', 'dense')), may hold values from 0 to 1
- table: float32 [32768, 128], P('owner'), may hold values from -6 to 6
- accum: float32 [32768], P('owner'), may hold values from 0.0001 to 0.01
- w_in: bfloat16 [1664, 4096], P(None, 'dense'), may hold values from -0.15625 to 0.15625
- b_in: bfloat16 [4096], P('dense'), may hold values from -3 to 3
- w_out: bfloat16 [4096], P('dense'), may hold values from -0.29882812 to 0.29882812
Outputs:
- new_table: float32 [32768, 128], P('owner')
- new_accum: float32 [32768], P('owner')
- weight_grad: float32 [8192, 13, 4], P(('owner', 'dense'))
Inputs may be any that keep to these rules, and one draw needn't show every extreme that they name: The 4 owners of one bag differ. Among the bags of one device (3328 of them, aligned blocks of rows), at most 1664 name one owner. Among the ids of one device's samples (13312 of them, aligned blocks of rows), exactly 416 distinct values of local_rows occur.
All inputs are finite; a program needn't handle non-finite values.
Results may differ from a plain program's by a relative error of at most 0.0056.
Values may be sent and summed in bfloat16 or wider, within the bound.
A program may use at most 128 MiB of HBM per device.

v0:
```python
import jax
import jax.numpy as jnp
from jax import lax
from jax.sharding import PartitionSpec as P

step_size = 0.5


def silu_slope(preact, sigma_pre):
    return sigma_pre * (1.0 + preact * (1.0 - sigma_pre))


def local(owners, local_rows, weights, labels, table, accum, w_in, b_in, w_out):
    samples, fields, bag_len = owners.shape
    emb_width = table.shape[1]
    table_rows = table.shape[0]
    groups = lax.axis_size("owner")
    slot_total = samples * fields * bag_len
    capacity = 2 * slot_total // groups
    own_flat = owners.reshape(slot_total)
    local_flat = local_rows.reshape(slot_total)
    owner_marks = (own_flat[None, :] == jnp.arange(groups, dtype=jnp.int32)[:, None]).astype(
        jnp.int32
    )
    earlier = jnp.cumsum(owner_marks, axis=1) - owner_marks
    slot_rank = jnp.sum(earlier * owner_marks, axis=0)
    slot_place = own_flat * capacity + slot_rank
    send_rows = jnp.zeros((groups * capacity,), jnp.int32).at[slot_place].set(local_flat)
    send_rows = send_rows.reshape(groups, capacity)
    asked_piece = lax.all_to_all(send_rows, "owner", split_axis=0, concat_axis=0, tiled=True)
    found_rows = table[asked_piece].astype(jnp.bfloat16)
    returned = lax.all_to_all(found_rows, "owner", split_axis=0, concat_axis=0, tiled=True)
    looked = returned.reshape(groups * capacity, emb_width)[slot_place]
    looked = looked.reshape(samples, fields, bag_len, emb_width)
    looked_f = looked.astype(jnp.float32)
    weight_sums = jnp.sum(weights, axis=-1)
    pooled = jnp.sum(weights[..., None] * looked_f, axis=2) / weight_sums[..., None]
    inputs = pooled.astype(jnp.bfloat16).reshape(samples, fields * emb_width)
    all_inputs, all_labels = (
        lax.all_gather(inputs, "dense", axis=0, tiled=True),
        lax.all_gather(labels, "dense", axis=0, tiled=True),
    )
    out_proj = w_out.astype(jnp.float32)
    preact = jnp.dot(all_inputs, w_in, preferred_element_type=jnp.float32) + b_in.astype(
        jnp.float32
    )
    sigma_pre = jax.nn.sigmoid(preact)
    partial_logits = jnp.sum(preact * sigma_pre * out_proj, axis=-1)
    logits = lax.psum(partial_logits, "dense")
    logit_grad = jax.nn.sigmoid(logits) - all_labels.astype(jnp.float32)
    dhidden = (logit_grad[:, None] * out_proj * silu_slope(preact, sigma_pre)).astype(jnp.bfloat16)
    dinputs = lax.psum_scatter(
        lax.dot_general(
            dhidden, w_in, (((1,), (1,)), ((), ())), preferred_element_type=jnp.float32
        ),
        "dense",
        scatter_dimension=0,
        tiled=True,
    )
    dpooled = dinputs.reshape(samples, fields, emb_width)
    along = jnp.sum(looked_f * dpooled[:, :, None, :], axis=-1)
    centre = jnp.sum(pooled * dpooled, axis=-1)
    weight_grad = (along - centre[..., None]) / weight_sums[..., None]
    slot_grad = ((weights / weight_sums[..., None])[..., None] * dpooled[:, :, None, :]).astype(
        jnp.bfloat16
    )
    slot_rows = slot_grad.reshape(slot_total, emb_width)
    send_grads = (
        jnp.zeros((groups * capacity, emb_width), jnp.bfloat16).at[slot_place].set(slot_rows)
    )
    send_grads = send_grads.reshape(groups, capacity, emb_width)
    got_grads = lax.all_to_all(send_grads, "owner", split_axis=0, concat_axis=0, tiled=True)
    row_part = (
        jnp.zeros((table_rows, emb_width), jnp.float32)
        .at[asked_piece.reshape(-1)]
        .add(got_grads.reshape(-1, emb_width).astype(jnp.float32))
    )
    row_grad = lax.psum(row_part.astype(jnp.bfloat16), "dense").astype(jnp.float32)
    new_accum = accum + jnp.mean(row_grad * row_grad, axis=-1)
    new_table = table - step_size * row_grad / jnp.sqrt(new_accum)[:, None]
    return (new_table, new_accum, weight_grad)


def solution(mesh):
    placed = (
        P(("owner", "dense"), None, None),
        P(("owner", "dense"), None, None),
        P(("owner", "dense"), None, None),
        P(("owner", "dense")),
        P("owner", None),
        P("owner"),
        P(None, "dense"),
        P("dense"),
        P("dense"),
    )
    return jax.shard_map(
        local,
        mesh=mesh,
        in_specs=placed,
        out_specs=(P("owner", None), P("owner"), P(("owner", "dense"), None, None)),
        check_vma=False,
    )
```

profile of v0, /device:TPU:0, one launch (start us, length us, event | category | flops | bytes accessed | tf_op | source)
XLA Modules:
  0.0 928.5 jit_solution(1450929109047367277)
XLA Ops:
  7.2 2.0 copy.32
  10.6 5.0 reduce-window.6
  20.6 49.2 %scatter_custom_fusion = s32[26624]{0:T(1024)S(1)} fusion(s32[13312]{0:T(1024)S(1)} %bitcast.33, s32[13312]{0:T(1024)S(1)} %reshape.200, s32[]{:T(128)} %constant.10.clone.1), kind=kCustom, calls=%fused_computation.42 | custom fusion | bytes 106500 | tf_op jit(solution)/shard_map/scatter | solution.py:28
  69.8 14.7 %all_to_all.22 = s32[16,1,1664]{2,1,0:T(1,128)S(1)} all-to-all(s32[16,1,1664]{2,1,0:T(1,128)S(1)} %bitcast.31), channel_id=1, replica_groups=mesh['owner'=16,'dense'=2] {'owner'}, dimensions={0} | all-to-all | bytes 212992 | tf_op jit(solution)/shard_map/all_to_all | solution.py:30
  84.6 88.9 %gather_fusion = bf16[26624,128]{1,0:T(8,128)(2,1)} fusion(f32[2048,128]{1,0:T(8,128)S(1)} %copy-done, s32[26624]{0:T(1024)S(1)} %broadcast_clamp_fusion), kind=kCustom, calls=%fused_computation | custom fusion | bytes 13737984 | tf_op jit(solution)/shard_map/gather | solution.py:31
  173.5 4.8 all-to-all-start.1
  179.7 121.7 %all-to-all-done.1 = bf16[16,1664,128]{2,1,0:T(8,128)(2,1)} async-done(((bf16[16,1664,128]{2,1,0:T(8,128)(2,1)}), bf16[16,1664,128]{2,1,0:T(8,128)(2,1)}, u32[]{:S(2)}, u32[]{:S(2)}) %all-to-all-start.1) | async-done | bytes 6815776 | tf_op jit(solution)/shard_map/all_to_all | solution.py:32
  301.4 48.6 %gather_fusion.1 = bf16[13312,128]{1,0:T(8,128)(2,1)} fusion(bf16[26624,128]{1,0:T(8,128)(2,1)} %bitcast.8, s32[13312]{0:T(1024)S(1)} %broadcast_clamp_fusion.1), kind=kCustom, calls=%fused_computation.1 | custom fusion | bytes 6868992 | tf_op jit(solution)/shard_map/gather | solution.py:33
  350.0 6.5 fusion.2
  358.5 1.6 copy.38
  360.3 4.4 all-gather
  364.7 49.8 %all-gather.3.cloned.1.call-done = bf16[512,1664]{0,1:T(8,128)(2,1)} async-done(((bf16[256,1664]{0,1:T(8,128)(2,1)}), bf16[512,1664]{0,1:T(8,128)(2,1)}) %all-gather.3.cloned.1.call-update) | async-done | bytes 1703952 | tf_op jit(solution)/shard_map/all_gather | solution.py:40
  414.5 10.2 %multiply_reduce_fusion = (f32[512]{0:T(512)S(1)}, f32[512,2048]{1,0:T(8,128)}) fusion(f32[2048]{0:T(1024)S(1)} %convert_element_type.60, f32[2048]{0:T(1024)S(1)} %convert_element_type.59, bf16[512,1664]{0,1:T(8,128)(2,1)} %all-gather.3.cloned.1.call-done, bf16[1664,2048]{1,0:T(8,128)(2,1)} %param.15), kind=kOutput, calls=%fused_computation.13 | convolution fusion | flops 3497000448 | bytes 12732416 | tf_op jit(solution)/shard_map/dot_general | solution.py:44
  424.6 4.9 psum.14
  429.5 11.1 %fusion.7 = f32[512,1664]{1,0:T(8,128)} fusion(bf16[1664,2048]{1,0:T(8,128)(2,1)} %param.15, f32[512,2048]{1,0:T(8,128)} %get-tuple-element.14, f32[512]{0:T(512)S(1)} %divide_subtract_fusion, f32[2048]{0:T(1024)S(1)} %convert_element_type.60, f32[2048]{0:T(1024)S(1)} %convert_element_type.59), kind=kOutput, calls=%fused_computation.18 | convolution fusion | flops 3501195264 | bytes 14436352 | tf_op jit(solution)/shard_map/dot_general | solution.py:53
  440.7 46.5 %reduce-scatter.2.cloned.1.call-done = f32[256,1664]{1,0:T(8,128)} async-done(((f32[512,1664]{1,0:T(8,128)}), f32[256,1664]{1,0:T(8,128)}) %reduce-scatter.2.cloned.1.call-update) | async-done | bytes 1703952 | tf_op jit(solution)/shard_map/reduce_scatter | solution.py:52
  487.1 2.9 copy.39
  490.1 2.2 copy.40
  492.3 2.5 multiply_reduce_fusion.1
  494.8 7.0 fusion.3
  501.8 4.2 subtract_divide_fusion
  506.0 2.1 mul.104
  508.1 4.0 mul.117
  512.1 44.7 %scatter_custom_fusion.1 = bf16[26624,128]{1,0:T(8,128)(2,1)} fusion(s32[13312]{0:T(1024)} %bitcast.35, f32[13312,128]{1,0:T(8,128)} %bitcast.25, f32[13312]{0:T(1024)S(1)} %mul.104, bf16[]{:T(256)} %constant.14.clone.1), kind=kCustom, calls=%fused_computation.15 | custom fusion | flops 3407872 | bytes 13685248 | tf_op jit(solution)/shard_map/scatter | solution.py:69
  556.9 5.7 all-to-all-start.2
  562.7 123.0 %all-to-all-done.2 = bf16[16,1664,128]{2,1,0:T(8,128)(2,1)} async-done(((bf16[16,1664,128]{2,1,0:T(8,128)(2,1)}), bf16[16,1664,128]{2,1,0:T(8,128)(2,1)}, u32[]{:S(2)}, u32[]{:S(2)}) %all-to-all-start.2) | async-done | bytes 6815776 | tf_op jit(solution)/shard_map/all_to_all | solution.py:72
  685.7 164.8 %scatter_custom_fusion.2 = f32[2048,128]{1,0:T(8,128)} fusion(s32[26624]{0:T(1024)S(1)} %bitcast.37, bf16[26624,128]{1,0:T(8,128)(2,1)} %bitcast.17, f32[]{:T(128)} %constant.9.clone.1), kind=kCustom, calls=%fused_computation.5 | custom fusion | flops 6815744 | bytes 7864324 | tf_op jit(solution)/shard_map/scatter-add | solution.py:76
  850.6 2.1 convert_element_type.66
  852.7 1.5 copy.42
  854.2 62.9 %all-reduce.2.cloned.1.call-done = bf16[2048,128]{1,0:T(8,128)(2,1)} async-done(((bf16[2048,128]{1,0:T(8,128)(2,1)}), bf16[2048,128]{1,0:T(8,128)(2,1)}) %all-reduce.2.cloned.1.call-update) | async-done | bytes 524304 | tf_op jit(solution)/shard_map/psum | solution.py:78
  917.2 1.4 fusion.14
  919.2 2.4 fusion.13
  (53 shorter events, 10.8 us)
Async XLA Ops:
  10.6 8.2 copy-start.6
  18.0 66.6 %copy-start = (f32[2048,128]{1,0:T(8,128)S(1)}, f32[2048,128]{1,0:T(8,128)}, u32[]{:S(2)}) copy-start(f32[2048,128]{1,0:T(8,128)} %param.13) | copy-start | bytes 3145732
  20.6 159.1 %copy-start.4 = (s32[13312,1]{0,1:T(1,128)}, s32[13312,1]{0,1:T(1,128)S(1)}, u32[]{:S(2)}) copy-start(s32[13312,1]{0,1:T(1,128)S(1)} %compare_select_fusion.2) | copy-start | bytes 159748
  173.5 4.8 copy-start.5
  173.5 127.9 %all-to-all-start.1 = ((bf16[16,1664,128]{2,1,0:T(8,128)(2,1)}), bf16[16,1664,128]{2,1,0:T(8,128)(2,1)}, u32[]{:S(2)}, u32[]{:S(2)}) async-start(bf16[16,1664,128]{2,1,0:T(8,128)(2,1)} %bitcast.27), calls=%async_computation.1 | async-start | bytes 13631488 | tf_op jit(solution)/shard_map/all_to_all | solution.py:32
  178.3 236.2 %all-gather.3.cloned.1.call-start = ((), (), s32[]{:S(2)}) async-start(), calls=%async_computation.4 | async-start | bytes 2555904 | tf_op jit(solution)/shard_map/all_gather | solution.py:40
  179.5 170.5 %copy-start.2 = (f32[256,13,4]{2,1,0:T(8,128)}, f32[256,13,4]{2,1,0:T(8,128)S(1)}, u32[]{:S(2)}) copy-start(f32[256,13,4]{2,1,0:T(8,128)S(1)} %copy.35) | copy-start | bytes 159748
  356.5 1.3 copy-start.1
  357.8 2.4 copy-start.8
  357.8 2.4 copy-start.9
  357.8 2.4 copy-start.10
  360.1 127.0 %reduce-scatter.2.cloned.1.call-start = ((), (), s32[]{:S(2)}) async-start(), calls=%async_computation.5 | async-start | bytes 5111808 | tf_op jit(solution)/shard_map/reduce_scatter | solution.py:52
  556.9 128.9 %all-to-all-start.2 = ((bf16[16,1664,128]{2,1,0:T(8,128)(2,1)}), bf16[16,1664,128]{2,1,0:T(8,128)(2,1)}, u32[]{:S(2)}, u32[]{:S(2)}) async-start(bf16[16,1664,128]{2,1,0:T(8,128)(2,1)} %bitcast.26), calls=%async_computation.3 | async-start | bytes 13631488 | tf_op jit(solution)/shard_map/all_to_all | solution.py:72
  562.5 354.6 %all-reduce.2.cloned.1.call-start = ((), (), s32[]{:S(2)}) async-start(), calls=%async_computation.6 | async-start | bytes 1048576 | tf_op jit(solution)/shard_map/psum | solution.py:78
  685.7 167.0 %copy-start.3 = (f32[256,13,4]{2,1,0:T(8,128)S(1)}, f32[256,13,4]{2,1,0:T(8,128)}, u32[]{:S(2)}) copy-start(f32[256,13,4]{2,1,0:T(8,128)} %get-tuple-element.11) | copy-start | bytes 159748
  850.6 68.0 %copy-start.7 = (f32[2048]{0:T(1024)S(1)}, f32[2048]{0:T(1024)}, u32[]{:S(2)}) copy-start(f32[2048]{0:T(1024)} %param.14) | copy-start | bytes 24580
Sparse Core Ops, SparseCore 0:
  360.3 54.1 all-gather.2
  440.8 46.2 reduce-scatter.1
  852.8 64.2 all-reduce.1
where the time goes:
time: 936 us; the launch traced here: 928 us
  waiting for transfers between devices  404 us (43%)
  other arithmetic  244 us (26%)
  local copies, waits for them, and re-layouts  210 us (22%)
  blocking collectives  24 us (3%)
  matrix products  21.3 us (2%)
  between operations  14.5 us (2%)
  starting transfers between devices  10.6 us (1%)
    scatter-add x1, other arithmetic, local(): row_part = jnp.zeros((table_rows, emb_width), jnp.float32).at[asked_piece...  165 us
    all_to_all x1, waiting for transfers between devices, local(): lax.all_to_all(send_grads, 'owner', split_axis=0, concat_axis=0, tiled=True)  123 us
    all_to_all x1, waiting for transfers between devices, local(): lax.all_to_all(found_rows, 'owner', split_axis=0, concat_axis=0, tiled=True)  122 us
    gather x1, local copies, waits for them, and re-layouts, local(): found_rows = table[asked_piece].astype(jnp.bfloat16)  88.9 us
    psum x1, waiting for transfers between devices, local(): lax.psum(row_part.astype(jnp.bfloat16), 'dense').astype(jnp.float32)  62.9 us
    all_gather x1, waiting for transfers between devices, local(): lax.all_gather(inputs, 'dense', axis=0, tiled=True)  49.8 us
    scatter x1, local copies, waits for them, and re-layouts, local(): jnp.zeros((groups * capacity,), jnp.int32).at[slot_place].set(local_flat)  49.2 us
    gather x1, local copies, waits for them, and re-layouts, local(): looked = returned.reshape(groups * capacity, emb_width)[slot_place]  48.6 us
  transfers between devices with their start and end apart: 5, of which 5 were waited for; matrix products, arithmetic and copies ran while one was open for 0% of the time, Pallas kernels for 0%

commit v1 on v0

v1 whole, which is shorter than its diff:
```python
import functools

import jax
import jax.numpy as jnp
from jax import lax
from jax.experimental import pallas as pl
from jax.experimental.pallas import tpu as pltpu
from jax.sharding import PartitionSpec as P

step_size = 0.5
lane = 128
f32 = jnp.float32
bf16 = jnp.bfloat16


def vmem():
    return pl.BlockSpec(memory_space=pltpu.VMEM)


def distinct_body(table_rows, own_ref, loc_ref, w_ref, uniq_ref, lo_ref, wo_ref):
    bag_len, bags = own_ref.shape
    groups = lo_ref.shape[0]
    uniq = uniq_ref.shape[0]
    highs = table_rows // lane
    counts = jnp.zeros((highs, lane), f32)
    owner_at = lax.broadcasted_iota(jnp.int32, (groups, bags), 0)
    low_at = lax.broadcasted_iota(jnp.int32, (lane, bags), 0)
    high_at = lax.broadcasted_iota(jnp.int32, (highs, bags), 0)
    named = jnp.full((groups, bags), -1, jnp.int32)
    weight = jnp.zeros((groups, bags), f32)
    for slot in range(bag_len):
        loc = loc_ref[slot : slot + 1, :]
        hit = own_ref[slot : slot + 1, :] == owner_at
        named = jnp.where(hit, loc, named)
        weight = jnp.where(hit, w_ref[slot : slot + 1, :], weight)
        low = jnp.where(jnp.bitwise_and(loc, lane - 1) == low_at, 1.0, 0.0).astype(bf16)
        high = jnp.where(jnp.right_shift(loc, 7) == high_at, 1.0, 0.0).astype(bf16)
        counts += lax.dot_general(high, low, (((1,), (1,)), ((), ())), preferred_element_type=f32)
    lo_ref[...] = named
    wo_ref[...] = weight
    present = jnp.where(counts > 0.0, 1.0, 0.0)
    upper = jnp.where(
        lax.broadcasted_iota(jnp.int32, (lane, lane), 0)
        <= lax.broadcasted_iota(jnp.int32, (lane, lane), 1),
        1.0,
        0.0,
    ).astype(bf16)
    inclusive = jnp.dot(present.astype(bf16), upper, preferred_element_type=f32)
    place = lax.broadcasted_iota(jnp.int32, (uniq, lane), 0).astype(f32)
    lane_at = lax.broadcasted_iota(jnp.int32, (1, lane), 1).astype(f32)
    before = jnp.zeros((1, 1), f32)
    found = jnp.zeros((uniq, lane), f32)
    for h in range(highs):
        here = present[h : h + 1, :]
        rank = jnp.where(here > 0.0, inclusive[h : h + 1, :] + before - 1.0, -1.0)
        found += jnp.where(place == rank, lane_at + float(h * lane), 0.0)
        before += jnp.sum(here, axis=1, keepdims=True)
    uniq_ref[...] = jnp.sum(found, axis=1, keepdims=True).astype(jnp.int32)


def lookup_body(list_ref, table_ref, out_ref):
    uniq = list_ref.shape[1]
    rows = table_ref.shape[0]
    at = lax.broadcasted_iota(jnp.int32, (uniq, rows), 1)
    pick = jnp.where(list_ref[0] == at, 1.0, 0.0).astype(bf16)
    out_ref[0] = jnp.dot(pick, table_ref[...], preferred_element_type=f32).astype(bf16)


def pool_body(uniq_ref, rows_ref, lo_ref, wo_ref, out_ref):
    groups = rows_ref.shape[0]
    named = lo_ref[...].T
    weight = wo_ref[...].T
    total = jnp.sum(weight, axis=1, keepdims=True)
    distinct = uniq_ref[...]
    acc = jnp.zeros(out_ref.shape, f32)
    for o in range(groups):
        mix = jnp.where(named[:, o : o + 1] == distinct, weight[:, o : o + 1], 0.0).astype(bf16)
        acc += jnp.dot(mix, rows_ref[o], preferred_element_type=f32)
    out_ref[...] = (acc / total).astype(bf16)


def backward_body(
    uniq_ref, rows_ref, lo_ref, wo_ref, own_ref, w_ref, dp_ref, grad_ref, wg_ref, acc, wide
):
    groups = rows_ref.shape[0]
    f = pl.program_id(0)

    @pl.when(f == 0)
    def _():
        acc[...] = jnp.zeros_like(acc)
        wide[...] = jnp.broadcast_to(uniq_ref[...], wide.shape)

    dp = dp_ref[...]
    dp_rows = dp.astype(bf16)
    dp_cols = dp.T.astype(bf16)
    slot_w = w_ref[...]
    own = own_ref[...]
    total = jnp.sum(slot_w, axis=0, keepdims=True)
    scaled = wo_ref[...] / total
    along = jnp.zeros(slot_w.shape, f32)
    for o in range(groups):
        hit = wide[...] == lo_ref[o : o + 1, :]
        mix = jnp.where(hit, scaled[o : o + 1, :], 0.0).astype(bf16)
        acc[o] += jnp.dot(mix, dp_rows, preferred_element_type=f32)
        dots = jnp.dot(rows_ref[o], dp_cols, preferred_element_type=f32)
        mine = jnp.sum(jnp.where(hit, dots, 0.0), axis=0, keepdims=True)
        along += jnp.where(own == o, mine, 0.0)
    centre = jnp.sum(slot_w * along, axis=0, keepdims=True) / total
    wg_ref[...] = (along - centre) / total

    @pl.when(f == pl.num_programs(0) - 1)
    def _():
        grad_ref[...] = acc[...].astype(bf16)


def collect_body(list_ref, got_ref, out_ref):
    groups, uniq = list_ref.shape
    rows = out_ref.shape[0]
    at = lax.broadcasted_iota(jnp.int32, (rows, uniq), 0) + pl.program_id(0) * rows
    acc = jnp.zeros(out_ref.shape, f32)
    for q in range(groups):
        pick = jnp.where(list_ref[q : q + 1, :] == at, 1.0, 0.0).astype(bf16)
        acc += jnp.dot(pick, got_ref[q], preferred_element_type=f32)
    out_ref[...] = acc.astype(bf16)


def head_pieces(w_in, b_in, w_out):
    groups = lax.axis_size("owner")
    parts = lax.axis_size("dense")
    half = w_in.shape[1] // 2
    core = lax.rem(lax.axis_index("owner"), 2)
    pieces = [(w_in, b_in, w_out)]
    mine = lax.dynamic_slice_in_dim(w_in, core * half, half, axis=1)
    swap = [(g, g + 1 - 2 * (g % 2)) for g in range(groups)]
    for shift in range(1, parts):
        ring = [(d, (d + shift) % parts) for d in range(parts)]
        w_here = lax.ppermute(mine, "dense", ring)
        b_all = lax.ppermute(b_in, "dense", ring)
        o_all = lax.ppermute(w_out, "dense", ring)
        w_there = lax.ppermute(w_here, "owner", swap)
        for w_piece, at in ((w_here, core * half), (w_there, (1 - core) * half)):
            pieces.append(
                (
                    w_piece,
                    lax.dynamic_slice_in_dim(b_all, at, half),
                    lax.dynamic_slice_in_dim(o_all, at, half),
                )
            )
    return pieces


def head(inputs, labels, pieces):
    kept = []
    logits = jnp.zeros((inputs.shape[0],), f32)
    for w, b, out in pieces:
        out = out.astype(f32)
        preact = jnp.dot(inputs, w, preferred_element_type=f32) + b.astype(f32)
        sigma = jax.nn.sigmoid(preact)
        logits += jnp.sum(preact * sigma * out, axis=-1)
        kept.append((w, out, preact, sigma))
    logit_grad = jax.nn.sigmoid(logits) - labels.astype(f32)
    dinputs = None
    for w, out, preact, sigma in kept:
        slope = sigma * (1.0 + preact * (1.0 - sigma))
        dhidden = (logit_grad[:, None] * out * slope).astype(bf16)
        term = lax.dot_general(dhidden, w, (((1,), (1,)), ((), ())), preferred_element_type=f32)
        dinputs = term if dinputs is None else dinputs + term
    return dinputs


def local(owners, local_rows, weights, labels, table, accum, w_in, b_in, w_out):
    samples, fields, bag_len = owners.shape
    table_rows, width = table.shape
    groups = lax.axis_size("owner")
    parts = lax.axis_size("dense")
    bags = samples * fields
    uniq = bags * bag_len // (2 * groups)
    pieces = head_pieces(w_in, b_in, w_out)

    def by_slot(x):
        return x.transpose(2, 1, 0).reshape(bag_len, bags)

    own, loc, w = by_slot(owners), by_slot(local_rows), by_slot(weights)
    distinct, named, spread = pl.pallas_call(
        functools.partial(distinct_body, table_rows),
        out_shape=(
            jax.ShapeDtypeStruct((uniq, 1), jnp.int32),
            jax.ShapeDtypeStruct((groups, bags), jnp.int32),
            jax.ShapeDtypeStruct((groups, bags), f32),
        ),
        in_specs=[vmem()] * 3,
        out_specs=(vmem(),) * 3,
        name="distinct",
    )(own, loc, w)
    distinct_row = distinct.reshape(1, uniq)
    lists = lax.all_gather(distinct_row, "owner", axis=0, tiled=True)
    found = pl.pallas_call(
        lookup_body,
        grid=(groups,),
        out_shape=jax.ShapeDtypeStruct((groups, uniq, width), bf16),
        in_specs=[pl.BlockSpec((1, uniq, 1), lambda q: (q, 0, 0)), vmem()],
        out_specs=pl.BlockSpec((1, uniq, width), lambda q: (q, 0, 0)),
        name="lookup",
    )(lists[:, :, None], table.astype(bf16))
    rows = lax.all_to_all(found, "owner", split_axis=0, concat_axis=0, tiled=True)

    block = pl.BlockSpec((groups, samples), lambda f: (0, f))
    slots = pl.BlockSpec((bag_len, samples), lambda f: (0, f))
    field = pl.BlockSpec((samples, width), lambda f: (0, f))
    inputs = pl.pallas_call(
        pool_body,
        grid=(fields,),
        out_shape=jax.ShapeDtypeStruct((samples, fields * width), bf16),
        in_specs=[vmem(), vmem(), block, block],
        out_specs=field,
        name="pool",
    )(distinct_row, rows, named, spread)

    dinputs = head(inputs, labels, pieces)

    grads, weight_grad = pl.pallas_call(
        backward_body,
        grid=(fields,),
        out_shape=(
            jax.ShapeDtypeStruct((groups, uniq, width), bf16),
            jax.ShapeDtypeStruct((bag_len, bags), f32),
        ),
        in_specs=[vmem(), vmem(), block, block, slots, slots, field],
        out_specs=(vmem(), slots),
        scratch_shapes=[
            pltpu.VMEM((groups, uniq, width), f32),
            pltpu.VMEM((uniq, samples), jnp.int32),
        ],
        name="backward",
    )(distinct, rows, named, spread, own, w, dinputs)
    weight_grad = weight_grad.reshape(bag_len, fields, samples).transpose(2, 1, 0)

    got = lax.all_to_all(grads, "owner", split_axis=0, concat_axis=0, tiled=True)
    chunk = table_rows // 8
    row_part = pl.pallas_call(
        collect_body,
        grid=(table_rows // chunk,),
        out_shape=jax.ShapeDtypeStruct((table_rows, width), bf16),
        in_specs=[vmem(), vmem()],
        out_specs=pl.BlockSpec((chunk, width), lambda r: (r, 0)),
        name="collect",
    )(lists, got)
    if parts == 2:
        other = lax.ppermute(row_part, "dense", [(0, 1), (1, 0)])
        row_grad = row_part.astype(f32) + other.astype(f32)
    else:
        row_grad = lax.psum(row_part, "dense").astype(f32)
    new_accum = accum + jnp.mean(row_grad * row_grad, axis=-1)
    new_table = table - step_size * row_grad / jnp.sqrt(new_accum)[:, None]
    return (new_table, new_accum, weight_grad)


def solution(mesh):
    placed = (
        P(("owner", "dense"), None, None),
        P(("owner", "dense"), None, None),
        P(("owner", "dense"), None, None),
        P(("owner", "dense")),
        P("owner", None),
        P("owner"),
        P(None, "dense"),
        P("dense"),
        P("dense"),
    )
    return jax.shard_map(
        local,
        mesh=mesh,
        in_specs=placed,
        out_specs=(P("owner", None), P("owner"), P(("owner", "dense"), None, None)),
        check_vma=False,
    )
```

time: 936 us -> 292 us (0.31)
  waiting for transfers between devices: 404 us -> 78.8 us
  other arithmetic: 244 us -> 6.29 us
  local copies, waits for them, and re-layouts: 210 us -> 14 us
  Pallas kernels: 0 us -> 83.3 us
  blocking collectives: 24 us -> 61.2 us
  between operations: 14.5 us -> 1.5 us
    all_to_all x2, waiting for transfers between devices: 245 us -> 62.9 us  [the longest x1 33.4 us: local(): lax.all_to_all(grads, 'owner', split_axis=0, concat_axis=0, tiled=True)]
    scatter-add x1 -> x0, other arithmetic: 165 us -> none  [local(): row_part = jnp.zeros((table_rows, emb_width), jnp.float32).at[asked_piece...]
    gather x2 -> x0, local copies, waits for them, and re-layouts: 137 us -> none  [the longest x1 88.9 us: local(): found_rows = table[asked_piece].astype(jnp.bfloat16)]
    pallas_call x0 -> x5, Pallas kernels: none -> 83.3 us  [the longest x1 30.3 us: local(): pl.pallas_call(backward_body, grid=(fields,), out_shape=(jax.ShapeDtypeSt...]
    psum x1 -> x0, waiting for transfers between devices: 62.9 us -> none  [local(): lax.psum(row_part.astype(jnp.bfloat16), 'dense').astype(jnp.float32)]
    unnamed x0 -> x1, blocking collectives: none -> 61.2 us
    all_gather x1 -> x0, waiting for transfers between devices: 49.8 us -> none  [local(): lax.all_gather(inputs, 'dense', axis=0, tiled=True)]
    scatter x1 -> x0, local copies, waits for them, and re-layouts: 49.2 us -> none  [local(): jnp.zeros((groups * capacity,), jnp.int32).at[slot_place].set(local_flat)]
  transfers between devices with their start and end apart: 5 -> 7, of which waited for: 5 -> 5; matrix products, arithmetic and copies ran while one was open for 0% -> 6% of each run, Pallas kernels for 0% -> 14%
where the time goes in v1:
time: 292 us; the launch traced here: 288 us
  Pallas kernels  83.3 us (29%)
  waiting for transfers between devices  78.8 us (27%)
  blocking collectives  61.2 us (21%)
  matrix products  23.5 us (8%)
  starting transfers between devices  19.6 us (7%)
  local copies, waits for them, and re-layouts  14 us (5%)
  other arithmetic  6.29 us (2%)
    unnamed x1, blocking collectives  61.2 us
    all_to_all x1, waiting for transfers between devices, local(): lax.all_to_all(grads, 'owner', split_axis=0, concat_axis=0, tiled=True)  33.4 us
    pallas_call x1, Pallas kernels, local(): pl.pallas_call(backward_body, grid=(fields,), out_shape=(jax.ShapeDtypeSt...  30.3 us
    all_to_all x1, waiting for transfers between devices, local(): lax.all_to_all(found, 'owner', split_axis=0, concat_axis=0, tiled=True)  29.5 us
    pallas_call x1, Pallas kernels, local(): pl.pallas_call(pool_body, grid=(fields,), out_shape=jax.ShapeDtypeStruct(...  22.9 us
    pallas_call x1, Pallas kernels, local(): pl.pallas_call(lookup_body, grid=(groups,), out_shape=jax.ShapeDtypeStruc...  14.7 us
    ppermute x1, waiting for transfers between devices, local(): other = lax.ppermute(row_part, 'dense', [(0, 1), (1, 0)])  13.7 us
    dot_general x3, matrix products, head(): preact = jnp.dot(inputs, w, preferred_element_type=f32) + b.astype(f32)  12.8 us
  transfers between devices with their start and end apart: 7, of which 5 were waited for; matrix products, arithmetic and copies ran while one was open for 6% of the time, Pallas kernels for 14%

profile of v1, /device:TPU:0, one launch (start us, length us, event | category | flops | bytes accessed | tf_op | source)
XLA Modules:
  0.0 288.1 jit_solution(13166993064329001954)
XLA Ops:
  0.7 4.1 %constant_dynamic-slice_fusion = bf16[1664,1024]{1,0:T(8,128)(2,1)} fusion(bf16[1664,2048]{1,0:T(8,128)(2,1)} %param.15, s32[]{:T(128)S(6)} %select_n.4), kind=kLoop, calls=%fused_computation.33 | loop fusion | bytes 6815748 | tf_op jit(solution)/shard_map/dynamic_slice | solution.py:133
  4.7 3.0 %collective-permute-start = (bf16[1664,1024]{1,0:T(8,128)(2,1)}, bf16[1664,1024]{1,0:T(8,128)(2,1)}, u32[]{:S(2)}, u32[]{:S(2)}) collective-permute-start(bf16[1664,1024]{1,0:T(8,128)(2,1)} %constant_dynamic-slice_fusion), channel_id=1, source_target_pairs={{0,1},{1,0},{2,3},{3,2},{4,5},{5,4},{6,7},{7,6},{8,9},{9,8},{10,11... | collective-permute-start | bytes 10223624 | tf_op jit(solution)/shard_map/ppermute | solution.py:137
  7.7 3.3 %distinct.1 = (s32[416,1]{1,0:T(8,128)}, s32[16,3328]{1,0:T(8,128)}, f32[16,3328]{1,0:T(8,128)}) custom-call(s32[4,3328]{1,0:T(4,128)} %bitcast.24, s32[4,3328]{1,0:T(4,128)} %bitcast.28, f32[4,3328]{1,0:T(4,128)} %bitcast.26), custom_call_target="tpu_custom_call" | custom-call | tf_op jit(solution)/shard_map/distinct/pallas_call | solution.py:184
  11.1 1.1 reduce
  13.7 61.2 %all-reduce = s32[6656]{0:T(1024)S(1)} all-reduce(s32[6656]{0:T(1024)S(1)} %dynamic-update-slice), channel_id=2, replica_groups=mesh['owner'=16,'dense'=2] {'owner'}, use_global_device_ids=true, to_apply=%add | all-reduce | flops 6656 | bytes 53248
  74.9 5.1 %broadcast_in_dim.3.list_ref = s32[16,416,1]{2,1,0:T(8,128)} reshape(s32[6656]{0:T(1024)S(1)} %all-reduce) | data formatting | bytes 53248 | tf_op jit(solution)/shard_map/broadcast_in_dim | solution.py:204
  80.0 0.8 convert_element_type.39.table_ref
  80.8 14.7 %lookup.1 = bf16[16,416,128]{2,1,0:T(8,128)(2,1)} custom-call(s32[16,416,1]{2,1,0:T(8,128)} %broadcast_in_dim.3.list_ref, bf16[2048,128]{1,0:T(8,128)(2,1)} %convert_element_type.39.table_ref), custom_call_target="tpu_custom_call" | custom-call | tf_op jit(solution)/shard_map/lookup/pallas_call | solution.py:197
  95.5 4.0 %all-to-all-start = ((bf16[16,416,128]{2,1,0:T(8,128)(2,1)}), bf16[16,416,128]{2,1,0:T(8,128)(2,1)S(1)}, u32[]{:S(2)}, u32[]{:S(2)}) async-start(bf16[16,416,128]{2,1,0:T(8,128)(2,1)} %lookup.1), calls=%async_computation | async-start | bytes 3407872 | tf_op jit(solution)/shard_map/all_to_all | solution.py:205
  99.7 0.6 collective-permute-start.2
  100.3 1.4 collective-permute-start.1
  101.8 1.6 collective-permute-done.2
  103.9 29.5 %all-to-all-done.rows_ref = bf16[16,416,128]{2,1,0:T(8,128)(2,1)S(1)} async-done(((bf16[16,416,128]{2,1,0:T(8,128)(2,1)}), bf16[16,416,128]{2,1,0:T(8,128)(2,1)S(1)}, u32[]{:S(2)}, u32[]{:S(2)}) %all-to-all-start) | async-done | bytes 1703968 | tf_op jit(solution)/shard_map/all_to_all | solution.py:205
  133.4 1.2 copy-done
  134.7 22.9 %pool.1 = bf16[256,1664]{1,0:T(8,128)(2,1)} custom-call(s32[1,416]{1,0:T(1,128)} %bitcast.29, bf16[16,416,128]{2,1,0:T(8,128)(2,1)} %copy-done, s32[16,3328]{1,0:T(8,128)} %get-tuple-element.9.lo_ref, f32[16,3328]{1,0:T(8,128)} %get-tuple-element.10.wo_ref), custom_call_target="tpu_custom_call" | custom-call | tf_op jit(solution)/shard_map/pool/pallas_call | solution.py:210
  157.5 5.7 %multiply_reduce_fusion = (f32[256]{0:T(256)S(1)}, f32[256,2048]{1,0:T(8,128)S(1)}) fusion(f32[2048]{0:T(1024)S(1)} %convert_element_type.41, f32[2048]{0:T(1024)S(1)} %convert_element_type.40, bf16[256,1664]{1,0:T(8,128)(2,1)} %pool.1, bf16[1664,2048]{1,0:T(8,128)(2,1)} %param.15), kind=kOutput, calls=%fused_computation.4 | convolution fusion | flops 1748500224 | bytes 9782272 | tf_op jit(solution)/shard_map/dot_general | solution.py:157
  163.3 3.5 %multiply_reduce_fusion.3 = (f32[256]{0:T(256)S(1)}, f32[256,1024]{1,0:T(8,128)S(1)}) fusion(f32[1024]{0:T(1024)S(1)} %get-tuple-element.18, f32[1024]{0:T(1024)S(1)} %get-tuple-element.20, bf16[256,1664]{1,0:T(8,128)(2,1)S(1)} %copy-done.3, bf16[1664,1024]{1,0:T(8,128)(2,1)} %collective-permute-done), kind=kOutput, calls=%fused_computation.17 | convolution fusion | flops 874249984 | bytes 5317632 | tf_op jit(solution)/shard_map/dot_general | solution.py:157
  166.8 3.5 %multiply_reduce_fusion.2 = (f32[256]{0:T(256)S(1)}, f32[256,1024]{1,0:T(8,128)S(1)}) fusion(f32[1024]{0:T(1024)S(1)} %get-tuple-element.19, f32[1024]{0:T(1024)S(1)} %get-tuple-element.21, bf16[256,1664]{1,0:T(8,128)(2,1)S(1)} %copy-done.3, bf16[1664,1024]{1,0:T(8,128)(2,1)} %collective-permute-done.3), kind=kOutput, calls=%fused_computation.15 | convolution fusion | flops 874249984 | bytes 5317632 | tf_op jit(solution)/shard_map/dot_general | solution.py:157
  170.4 2.7 fusion
  173.1 3.4 %convolution_add_fusion.1 = f32[256,1664]{1,0:T(8,128)S(1)} fusion(f32[256,1664]{1,0:T(8,128)S(1)} %fusion, bf16[1664,1024]{1,0:T(8,128)(2,1)} %collective-permute-done, f32[256,1024]{1,0:T(8,128)S(1)} %get-tuple-element.27, f32[256]{0:T(256)S(1)} %divide_subtract_fusion.1, f32[1024]{0:T(1024)S(1)} %get-tuple-element.18), kind=kOutput, calls=%fused_computation.1 | convolution fusion | flops 875462656 | bytes 7869440 | tf_op jit(solution)/shard_map/dot_general | solution.py:166
  176.5 4.7 %convolution_add_fusion.dp_ref = f32[256,1664]{1,0:T(8,128)} fusion(f32[256,1664]{1,0:T(8,128)S(1)} %convolution_add_fusion.1, bf16[1664,1024]{1,0:T(8,128)(2,1)} %collective-permute-done.3, f32[256,1024]{1,0:T(8,128)S(1)} %get-tuple-element.23, f32[256]{0:T(256)S(1)} %divide_subtract_fusion.1, f32[1024]{0:T(1024)S(1)} %get-tuple-element.19), kind=kOutput, calls=%fused_computation | convolution fusion | flops 875462656 | bytes 7869440 | tf_op jit(solution)/shard_map/dot_general | solution.py:166
  181.2 30.3 %backward.1 = (bf16[16,416,128]{2,1,0:T(8,128)(2,1)}, f32[4,3328]{1,0:T(4,128)}) custom-call(s32[416,1]{1,0:T(8,128)} %get-tuple-element.8.uniq_ref, bf16[16,416,128]{2,1,0:T(8,128)(2,1)} %copy-done, s32[16,3328]{1,0:T(8,128)} %get-tuple-element.9.lo_ref, f32[16,3328]{1,0:T(8,128)} %get-tuple-element.10.wo_ref, s32[4,3328]{1,0:T(4,128)} %bitcast.25, ...), custom_call_target="tpu_custom_call" | custom-call | tf_op jit(solution)/shard_map/backward/pallas_call | solution.py:221
  211.5 9.7 %all-to-all-start.1 = ((bf16[16,416,128]{2,1,0:T(8,128)(2,1)}), bf16[16,416,128]{2,1,0:T(8,128)(2,1)S(1)}, u32[]{:S(2)}, u32[]{:S(2)}) async-start(bf16[16,416,128]{2,1,0:T(8,128)(2,1)} %get-tuple-element.11), calls=%async_computation.1 | async-start | bytes 3407872 | tf_op jit(solution)/shard_map/all_to_all | solution.py:238
  221.3 0.7 reshape.34.list_ref
  222.0 33.4 %all-to-all-done.1.got_ref = bf16[16,416,128]{2,1,0:T(8,128)(2,1)S(1)} async-done(((bf16[16,416,128]{2,1,0:T(8,128)(2,1)}), bf16[16,416,128]{2,1,0:T(8,128)(2,1)S(1)}, u32[]{:S(2)}, u32[]{:S(2)}) %all-to-all-start.1) | async-done | bytes 1703968 | tf_op jit(solution)/shard_map/all_to_all | solution.py:238
  255.4 1.2 copy-done.1
  256.6 12.2 %collect.1 = bf16[2048,128]{1,0:T(8,128)(2,1)} custom-call(s32[16,416]{1,0:T(8,128)} %reshape.34.list_ref, bf16[16,416,128]{2,1,0:T(8,128)(2,1)} %copy-done.1), custom_call_target="tpu_custom_call" | custom-call | tf_op jit(solution)/shard_map/collect/pallas_call | solution.py:240
  269.4 0.7 copy.14
  270.0 13.7 %collective-permute-done.4 = bf16[2048,128]{1,0:T(8,128)(2,1)S(1)} collective-permute-done((bf16[2048,128]{1,0:T(8,128)(2,1)}, bf16[2048,128]{1,0:T(8,128)(2,1)S(1)}, u32[]{:S(2)}, u32[]{:S(2)}) %collective-permute-start.4) | collective-permute-done | bytes 524320 | tf_op jit(solution)/shard_map/ppermute | solution.py:249
  283.8 1.4 multiply_reduce_fusion.1
  285.2 0.6 fusion.13
  285.8 2.4 divide_subtract_fusion
  (39 shorter events, 2.4 us)
Async XLA Ops:
  0.6 11.5 %copy-start.10 = (u32[32]{0:T(128)S(1)}, u32[32]{0:T(128)}, u32[]{:S(2)}) copy-start(u32[32]{0:T(128)} %constant.30) | copy-start | bytes 388
  4.7 75.2 %copy-start.2 = (f32[2048,128]{1,0:T(8,128)S(1)}, f32[2048,128]{1,0:T(8,128)}, u32[]{:S(2)}) copy-start(f32[2048,128]{1,0:T(8,128)} %param.13) | copy-start | bytes 3145732
  4.7 94.8 %collective-permute-start = (bf16[1664,1024]{1,0:T(8,128)(2,1)}, bf16[1664,1024]{1,0:T(8,128)(2,1)}, u32[]{:S(2)}, u32[]{:S(2)}) collective-permute-start(bf16[1664,1024]{1,0:T(8,128)(2,1)} %constant_dynamic-slice_fusion), channel_id=1, source_target_pairs={{0,1},{1,0},{2,3},{3,2},{4,5},{5,4},{6,7},{7,6},{8,9},{9,8},{10,11... | collective-permute-start | bytes 10223624 | tf_op jit(solution)/shard_map/ppermute | solution.py:137
  12.1 68.7 %copy-start.5 = (s32[416]{0:T(512)}, s32[416]{0:T(512)S(1)}, u32[]{:S(2)}) copy-start(s32[416]{0:T(512)S(1)} %reduce) | copy-start | bytes 4996
  95.5 4.2 %copy-start.7 = (bf16[2048]{0:T(1024)(128)(2,1)S(1)}, bf16[2048]{0:T(1024)(128)(2,1)}, u32[]{:S(2)}) copy-start(bf16[2048]{0:T(1024)(128)(2,1)} %param.17) | copy-start | bytes 12292
  95.5 4.8 %copy-start.8 = (bf16[2048]{0:T(1024)(128)(2,1)S(1)}, bf16[2048]{0:T(1024)(128)(2,1)}, u32[]{:S(2)}) copy-start(bf16[2048]{0:T(1024)(128)(2,1)} %param.16) | copy-start | bytes 12292
  95.5 37.9 %all-to-all-start = ((bf16[16,416,128]{2,1,0:T(8,128)(2,1)}), bf16[16,416,128]{2,1,0:T(8,128)(2,1)S(1)}, u32[]{:S(2)}, u32[]{:S(2)}) async-start(bf16[16,416,128]{2,1,0:T(8,128)(2,1)} %lookup.1), calls=%async_computation | async-start | bytes 3407872 | tf_op jit(solution)/shard_map/all_to_all | solution.py:205
  99.5 67.2 %collective-permute-start.3 = (bf16[1664,1024]{1,0:T(8,128)(2,1)}, bf16[1664,1024]{1,0:T(8,128)(2,1)}, u32[]{:S(2)}, u32[]{:S(2)}) collective-permute-start(bf16[1664,1024]{1,0:T(8,128)(2,1)} %collective-permute-done), channel_id=1, source_target_pairs={{0,2},{2,0},{4,6},{6,4},{8,10},{10,8},{12,14},{14,12},{16,18},{18,... | collective-permute-start | bytes 10223624 | tf_op jit(solution)/shard_map/ppermute | solution.py:140
  99.7 3.6 %collective-permute-start.2 = (bf16[2048]{0:T(1024)(128)(2,1)S(1)}, bf16[2048]{0:T(1024)(128)(2,1)S(1)}, u32[]{:S(2)}, u32[]{:S(2)}) collective-permute-start(bf16[2048]{0:T(1024)(128)(2,1)S(1)} %copy-done.7), channel_id=1, source_target_pairs={{0,1},{1,0},{2,3},{3,2},{4,5},{5,4},{6,7},{7,6},{8,9},{9,8},{10,11... | collective-permute-start | bytes 12296 | tf_op jit(solution)/shard_map/ppermute | solution.py:139
  100.3 3.6 %collective-permute-start.1 = (bf16[2048]{0:T(1024)(128)(2,1)S(1)}, bf16[2048]{0:T(1024)(128)(2,1)S(1)}, u32[]{:S(2)}, u32[]{:S(2)}) collective-permute-start(bf16[2048]{0:T(1024)(128)(2,1)S(1)} %copy-done.8), channel_id=1, source_target_pairs={{0,1},{1,0},{2,3},{3,2},{4,5},{5,4},{6,7},{7,6},{8,9},{9,8},{10,11... | collective-permute-start | bytes 12296 | tf_op jit(solution)/shard_map/ppermute | solution.py:138
  133.4 1.2 copy-start
  157.5 5.7 %copy-start.3 = (bf16[256,1664]{1,0:T(8,128)(2,1)S(1)}, bf16[256,1664]{1,0:T(8,128)(2,1)}, u32[]{:S(2)}) copy-start(bf16[256,1664]{1,0:T(8,128)(2,1)} %pool.1) | copy-start | bytes 2555908
  163.2 7.1 %slice-start = ((s8[6815744]{0:T(1024)(128)(4,1)}), s8[4194304]{0:T(1024)(128)(4,1)S(1)}, s32[]{:S(2)}) async-start(s8[6815744]{0:T(1024)(128)(4,1)} %bitcast.21), calls=%async_computation.2 | async-start | bytes 8388608
  166.8 3.5 %copy-start.9 = (bf16[256]{0:T(256)(128)(2,1)S(1)}, bf16[256]{0:T(256)(128)(2,1)}, u32[]{:S(2)}) copy-start(bf16[256]{0:T(256)(128)(2,1)} %param.12) | copy-start | bytes 1540
  166.8 3.6 %slice-start.1 = ((s8[6815744]{0:T(1024)(128)(4,1)}), s8[2621440]{0:T(1024)(128)(4,1)S(1)}, s32[]{:S(2)}) async-start(s8[6815744]{0:T(1024)(128)(4,1)} %bitcast.21), calls=%async_computation.3 | async-start | bytes 5242880
  211.5 57.9 %copy-start.4 = (f32[4,3328]{1,0:T(4,128)S(1)}, f32[4,3328]{1,0:T(4,128)}, u32[]{:S(2)}) copy-start(f32[4,3328]{1,0:T(4,128)} %get-tuple-element.12) | copy-start | bytes 159748
  211.5 43.9 %all-to-all-start.1 = ((bf16[16,416,128]{2,1,0:T(8,128)(2,1)}), bf16[16,416,128]{2,1,0:T(8,128)(2,1)S(1)}, u32[]{:S(2)}, u32[]{:S(2)}) async-start(bf16[16,416,128]{2,1,0:T(8,128)(2,1)} %get-tuple-element.11), calls=%async_computation.1 | async-start | bytes 3407872 | tf_op jit(solution)/shard_map/all_to_all | solution.py:238
  221.2 63.9 %copy-start.6 = (f32[2048]{0:T(1024)S(1)}, f32[2048]{0:T(1024)}, u32[]{:S(2)}) copy-start(f32[2048]{0:T(1024)} %param.14) | copy-start | bytes 24580
  255.4 1.2 copy-start.1
  268.7 15.0 %collective-permute-start.4 = (bf16[2048,128]{1,0:T(8,128)(2,1)}, bf16[2048,128]{1,0:T(8,128)(2,1)S(1)}, u32[]{:S(2)}, u32[]{:S(2)}) collective-permute-start(bf16[2048,128]{1,0:T(8,128)(2,1)} %collect.1), channel_id=1, source_target_pairs={{0,1},{1,0},{2,3},{3,2},{4,5},{5,4},{6,7},{7,6},{8,9},{9,8},{10,11... | collective-permute-start | bytes 1572872 | tf_op jit(solution)/shard_map/ppermute | solution.py:249

commit v2 on v1

--- a/solution.py
+++ b/solution.py
@@ -17,10 +17,11 @@
     return pl.BlockSpec(memory_space=pltpu.VMEM)
 
 
-def distinct_body(table_rows, own_ref, loc_ref, w_ref, uniq_ref, lo_ref, wo_ref):
+def distinct_body(table_rows, own_ref, loc_ref, w_ref, uniq_ref, row_ref, lo_ref, wo_ref):
     bag_len, bags = own_ref.shape
     groups = lo_ref.shape[0]
     uniq = uniq_ref.shape[0]
+    padded = row_ref.shape[1]
     highs = table_rows // lane
     counts = jnp.zeros((highs, lane), f32)
     owner_at = lax.broadcasted_iota(jnp.int32, (groups, bags), 0)
@@ -46,24 +47,67 @@
         0.0,
     ).astype(bf16)
     inclusive = jnp.dot(present.astype(bf16), upper, preferred_element_type=f32)
-    place = lax.broadcasted_iota(jnp.int32, (uniq, lane), 0).astype(f32)
+    place = lax.broadcasted_iota(jnp.int32, (padded, lane), 0).astype(f32)
     lane_at = lax.broadcasted_iota(jnp.int32, (1, lane), 1).astype(f32)
     before = jnp.zeros((1, 1), f32)
-    found = jnp.zeros((uniq, lane), f32)
+    found = jnp.where(place < float(uniq), 0.0, -1.0)
     for h in range(highs):
         here = present[h : h + 1, :]
         rank = jnp.where(here > 0.0, inclusive[h : h + 1, :] + before - 1.0, -1.0)
         found += jnp.where(place == rank, lane_at + float(h * lane), 0.0)
         before += jnp.sum(here, axis=1, keepdims=True)
-    uniq_ref[...] = jnp.sum(found, axis=1, keepdims=True).astype(jnp.int32)
-
-
-def lookup_body(list_ref, table_ref, out_ref):
-    uniq = list_ref.shape[1]
-    rows = table_ref.shape[0]
-    at = lax.broadcasted_iota(jnp.int32, (uniq, rows), 1)
-    pick = jnp.where(list_ref[0] == at, 1.0, 0.0).astype(bf16)
-    out_ref[0] = jnp.dot(pick, table_ref[...], preferred_element_type=f32).astype(bf16)
+    column = jnp.sum(found, axis=1, keepdims=True)
+    uniq_ref[...] = column[:uniq].astype(jnp.int32)
+    row_ref[...] = jnp.broadcast_to(column, (padded, lane)).T[0:1].astype(jnp.int32)
+
+
+def share_body(groups, row_ref, out_ref, send_sem, recv_sem, own_sem):
+    me = lax.axis_index("owner")
+    barrier = pltpu.get_barrier_semaphore()
+    for k in range(1, groups):
+        peer = lax.rem(me + k, groups)
+        pl.semaphore_signal(
+            barrier, inc=1, device_id={"owner": peer}, device_id_type=pl.DeviceIdType.MESH
+        )
+    pl.semaphore_wait(barrier, groups - 1)
+    copies = []
+    for k in range(1, groups):
+        copies.append(
+            pltpu.make_async_remote_copy(
+                src_ref=row_ref,
+                dst_ref=out_ref.at[me],
+                send_sem=send_sem.at[k],
+                recv_sem=recv_sem.at[k],
+                device_id={"owner": lax.rem(me + k, groups)},
+                device_id_type=pl.DeviceIdType.MESH,
+            )
+        )
+    for copy in copies:
+        copy.start()
+    mine = pltpu.make_async_copy(row_ref, out_ref.at[me], own_sem)
+    mine.start()
+    mine.wait()
+    for copy in copies:
+        copy.wait()
+
+
+def lookup_body(list_ref, table_ref, out_ref, wide, columns):
+    groups, uniq, width = out_ref.shape
+    depth = wide.shape[0]
+    folds = table_ref.shape[0] // depth
+    for j in range(folds):
+        wide[:, j * width : (j + 1) * width] = table_ref[j * depth : (j + 1) * depth, :].astype(bf16)
+    columns[...] = list_ref[...].T
+    at = lax.broadcasted_iota(jnp.int32, (uniq, depth), 1)
+    for q in range(groups):
+        ids = columns[:uniq, q : q + 1]
+        fold = ids // depth
+        pick = jnp.where(ids - fold * depth == at, 1.0, 0.0).astype(bf16)
+        every = jnp.dot(pick, wide[...], preferred_element_type=f32)
+        row = every[:, :width]
+        for j in range(1, folds):
+            row = jnp.where(fold == j, every[:, j * width : (j + 1) * width], row)
+        out_ref[q] = row.astype(bf16)
 
 
 def pool_body(uniq_ref, rows_ref, lo_ref, wo_ref, out_ref):
@@ -113,15 +157,27 @@
         grad_ref[...] = acc[...].astype(bf16)
 
 
-def collect_body(list_ref, got_ref, out_ref):
-    groups, uniq = list_ref.shape
-    rows = out_ref.shape[0]
-    at = lax.broadcasted_iota(jnp.int32, (rows, uniq), 0) + pl.program_id(0) * rows
-    acc = jnp.zeros(out_ref.shape, f32)
+def collect_body(base, list_ref, got_ref, out_ref, columns, acc):
+    groups, uniq, width = got_ref.shape
+    half = out_ref.shape[0] // 2
+    columns[...] = list_ref[...].T - base
+    at = lax.broadcasted_iota(jnp.int32, (half, uniq), 0)
     for q in range(groups):
-        pick = jnp.where(list_ref[q : q + 1, :] == at, 1.0, 0.0).astype(bf16)
-        acc += jnp.dot(pick, got_ref[q], preferred_element_type=f32)
-    out_ref[...] = acc.astype(bf16)
+        row = list_ref[q : q + 1, :uniq] - base
+        row = jnp.where(row >= half, row - half, row)
+        pick = jnp.where(row == at, 1.0, 0.0).astype(bf16)
+        ids = columns[:uniq, q : q + 1]
+        got = got_ref[q].astype(f32)
+        first = jnp.where(ids < half, got, 0.0)
+        second = jnp.where(ids >= half, got, 0.0)
+        both = jnp.concatenate([first, second], axis=1).astype(bf16)
+        term = jnp.dot(pick, both, preferred_element_type=f32)
+        if q == 0:
+            acc[...] = term
+        else:
+            acc[...] += term
+    out_ref[:half] = acc[:, :width].astype(bf16)
+    out_ref[half:] = acc[:, width:].astype(bf16)
 
 
 def head_pieces(w_in, b_in, w_out):
@@ -175,33 +231,51 @@
     parts = lax.axis_size("dense")
     bags = samples * fields
     uniq = bags * bag_len // (2 * groups)
-    pieces = head_pieces(w_in, b_in, w_out)
+    padded = -(-uniq // lane) * lane
 
     def by_slot(x):
         return x.transpose(2, 1, 0).reshape(bag_len, bags)
 
     own, loc, w = by_slot(owners), by_slot(local_rows), by_slot(weights)
-    distinct, named, spread = pl.pallas_call(
+    distinct, distinct_row, named, spread = pl.pallas_call(
         functools.partial(distinct_body, table_rows),
         out_shape=(
             jax.ShapeDtypeStruct((uniq, 1), jnp.int32),
+            jax.ShapeDtypeStruct((1, padded), jnp.int32),
             jax.ShapeDtypeStruct((groups, bags), jnp.int32),
             jax.ShapeDtypeStruct((groups, bags), f32),
         ),
         in_specs=[vmem()] * 3,
-        out_specs=(vmem(),) * 3,
+        out_specs=(vmem(),) * 4,
         name="distinct",
     )(own, loc, w)
-    distinct_row = distinct.reshape(1, uniq)
-    lists = lax.all_gather(distinct_row, "owner", axis=0, tiled=True)
+    lists = pl.pallas_call(
+        functools.partial(share_body, groups),
+        out_shape=jax.ShapeDtypeStruct((groups, 1, padded), jnp.int32),
+        in_specs=[vmem()],
+        out_specs=vmem(),
+        scratch_shapes=[
+            pltpu.SemaphoreType.DMA((groups,)),
+            pltpu.SemaphoreType.DMA((groups,)),
+            pltpu.SemaphoreType.DMA,
+        ],
+        compiler_params=pltpu.CompilerParams(collective_id=0, has_side_effects=True),
+        name="share",
+    )(distinct_row).reshape(groups, padded)
+    lists, w_later = lax.optimization_barrier((lists, w_in))
+    pieces = head_pieces(w_later, b_in, w_out)
+    depth = table_rows // 4
     found = pl.pallas_call(
         lookup_body,
-        grid=(groups,),
         out_shape=jax.ShapeDtypeStruct((groups, uniq, width), bf16),
-        in_specs=[pl.BlockSpec((1, uniq, 1), lambda q: (q, 0, 0)), vmem()],
-        out_specs=pl.BlockSpec((1, uniq, width), lambda q: (q, 0, 0)),
+        in_specs=[vmem(), vmem()],
+        out_specs=vmem(),
+        scratch_shapes=[
+            pltpu.VMEM((depth, 4 * width), bf16),
+            pltpu.VMEM((padded, groups), jnp.int32),
+        ],
         name="lookup",
-    )(lists[:, :, None], table.astype(bf16))
+    )(lists, table)
     rows = lax.all_to_all(found, "owner", split_axis=0, concat_axis=0, tiled=True)
 
     block = pl.BlockSpec((groups, samples), lambda f: (0, f))
@@ -214,7 +288,7 @@
         in_specs=[vmem(), vmem(), block, block],
         out_specs=field,
         name="pool",
-    )(distinct_row, rows, named, spread)
+    )(distinct_row[:, :uniq], rows, named, spread)
 
     dinputs = head(inputs, labels, pieces)
 
@@ -236,20 +310,26 @@
     weight_grad = weight_grad.reshape(bag_len, fields, samples).transpose(2, 1, 0)
 
     got = lax.all_to_all(grads, "owner", split_axis=0, concat_axis=0, tiled=True)
-    chunk = table_rows // 8
-    row_part = pl.pallas_call(
-        collect_body,
-        grid=(table_rows // chunk,),
-        out_shape=jax.ShapeDtypeStruct((table_rows, width), bf16),
-        in_specs=[vmem(), vmem()],
-        out_specs=pl.BlockSpec((chunk, width), lambda r: (r, 0)),
-        name="collect",
-    )(lists, got)
-    if parts == 2:
-        other = lax.ppermute(row_part, "dense", [(0, 1), (1, 0)])
-        row_grad = row_part.astype(f32) + other.astype(f32)
-    else:
-        row_grad = lax.psum(row_part, "dense").astype(f32)
+    chunk = table_rows // 2
+    sums = []
+    for base in range(0, table_rows, chunk):
+        row_part = pl.pallas_call(
+            functools.partial(collect_body, base),
+            out_shape=jax.ShapeDtypeStruct((chunk, width), bf16),
+            in_specs=[vmem(), vmem()],
+            out_specs=vmem(),
+            scratch_shapes=[
+                pltpu.VMEM((padded, groups), jnp.int32),
+                pltpu.VMEM((chunk // 2, 2 * width), f32),
+            ],
+            name="collect",
+        )(lists, got)
+        if parts == 2:
+            other = lax.ppermute(row_part, "dense", [(0, 1), (1, 0)])
+            sums.append(row_part.astype(f32) + other.astype(f32))
+        else:
+            sums.append(lax.psum(row_part, "dense").astype(f32))
+    row_grad = jnp.concatenate(sums, axis=0)
     new_accum = accum + jnp.mean(row_grad * row_grad, axis=-1)
     new_table = table - step_size * row_grad / jnp.sqrt(new_accum)[:, None]
     return (new_table, new_accum, weight_grad)

time: 292 us -> 249 us (0.85); the launches traced: 288 us -> 248 us
  blocking collectives: 61.2 us -> 46.4 us
  waiting for transfers between devices: 78.8 us -> 70.2 us
  starting transfers between devices: 19.6 us -> 11.3 us
  local copies, waits for them, and re-layouts: 14 us -> 7.44 us
  other arithmetic: 6.29 us -> 3.35 us
    unnamed x1 -> x0, blocking collectives: 61.2 us -> none
    ppermute x1, waiting for transfers between devices: 0.01 us -> 61 us  [head_pieces(): w_here = lax.ppermute(mine, 'dense', ring)]
    all_to_all x0 -> x1, blocking collectives: none -> 46.4 us  [local(): lax.all_to_all(grads, 'owner', split_axis=0, concat_axis=0, tiled=True)]
    all_to_all x1 -> x0, waiting for transfers between devices: 33.4 us -> none  [local(): lax.all_to_all(grads, 'owner', split_axis=0, concat_axis=0, tiled=True)]
    all_to_all x1, waiting for transfers between devices: 29.5 us -> 0.01 us  [local(): lax.all_to_all(found, 'owner', split_axis=0, concat_axis=0, tiled=True)]
    all_to_all x1 -> x0, starting transfers between devices: 9.75 us -> none  [local(): lax.all_to_all(grads, 'owner', split_axis=0, concat_axis=0, tiled=True)]
    ppermute x1 -> x2, waiting for transfers between devices: 13.7 us -> 6.06 us  [local(): other = lax.ppermute(row_part, 'dense', [(0, 1), (1, 0)])]
    broadcast_in_dim x1 -> x0, local copies, waits for them, and re-layouts: 5.11 us -> none  [local(): lists[:, :, None]]
  transfers between devices with their start and end apart: 7 -> 7, of which waited for: 5 -> 5; matrix products, arithmetic and copies ran while one was open for 6% -> 4% of each run, Pallas kernels for 14% -> 15%
where the time goes in v2:
time: 249 us; the launch traced here: 248 us
  Pallas kernels  85.4 us (34%)
  waiting for transfers between devices  70.2 us (28%)
  blocking collectives  46.4 us (19%)
  matrix products  23.5 us (9%)
  starting transfers between devices  11.3 us (5%)
  local copies, waits for them, and re-layouts  7.44 us (3%)
  other arithmetic  3.35 us (1%)
    ppermute x1, waiting for transfers between devices, head_pieces(): w_here = lax.ppermute(mine, 'dense', ring)  61 us
    all_to_all x1, blocking collectives, local(): lax.all_to_all(grads, 'owner', split_axis=0, concat_axis=0, tiled=True)  46.4 us
    pallas_call x1, Pallas kernels, local(): pl.pallas_call(backward_body, grid=(fields,), out_shape=(jax.ShapeDtypeSt...  30.3 us
    pallas_call x1, Pallas kernels, local(): pl.pallas_call(pool_body, grid=(fields,), out_shape=jax.ShapeDtypeStruct(...  22.9 us
    dot_general x3, matrix products, head(): preact = jnp.dot(inputs, w, preferred_element_type=f32) + b.astype(f32)  12.7 us
    pallas_call x2, Pallas kernels, local(): pl.pallas_call(functools.partial(collect_body, base), out_shape=jax.Shape...  11 us
    dot_general x3, matrix products, head(): lax.dot_general(dhidden, w, (((1,), (1,)), ((), ())), preferred_element_t...  10.8 us
    pallas_call x1, Pallas kernels, local(): pl.pallas_call(functools.partial(share_body, groups), out_shape=jax.Shape...  9.91 us
  transfers between devices with their start and end apart: 7, of which 5 were waited for; matrix products, arithmetic and copies ran while one was open for 4% of the time, Pallas kernels for 15%

profile of v2, /device:TPU:0, one launch (start us, length us, event | category | flops | bytes accessed | tf_op | source)
XLA Modules:
  0.0 248.3 jit_solution(18266923328407844276)
XLA Ops:
  0.6 3.5 %distinct.1 = (s32[416,1]{1,0:T(8,128)}, s32[1,512]{1,0:T(1,128)}, s32[16,3328]{1,0:T(8,128)}, f32[16,3328]{1,0:T(8,128)}) custom-call(s32[4,3328]{1,0:T(4,128)} %bitcast.29, s32[4,3328]{1,0:T(4,128)} %bitcast.33, f32[4,3328]{1,0:T(4,128)} %bitcast.31), custom_call_target="tpu_custom_call" | custom-call | tf_op jit(solution)/shard_map/distinct/pallas_call | solution.py:240
  4.2 9.9 %share.1 = s32[16,1,512]{2,1,0:T(1,128)} custom-call(s32[1,512]{1,0:T(1,128)} %get-tuple-element.11.row_ref), custom_call_target="tpu_custom_call" | custom-call | tf_op jit(solution)/shard_map/share/pallas_call | solution.py:252
  14.1 1.4 copy.16
  15.5 4.1 %constant_dynamic-slice_fusion = bf16[1664,1024]{1,0:T(8,128)(2,1)} fusion(bf16[1664,2048]{1,0:T(8,128)(2,1)} %param.15, s32[]{:T(128)S(6)} %select_n.4), kind=kLoop, calls=%fused_computation.36 | loop fusion | bytes 6815748 | tf_op jit(solution)/shard_map/dynamic_slice | solution.py:189
  19.5 1.5 collective-permute-start
  21.0 7.8 %lookup.1 = bf16[16,416,128]{2,1,0:T(8,128)(2,1)} custom-call(s32[16,512]{1,0:T(8,128)} %bitcast.25, f32[2048,128]{1,0:T(8,128)} %table_ref.1), custom_call_target="tpu_custom_call" | custom-call | tf_op jit(solution)/shard_map/lookup/pallas_call | solution.py:268
  28.9 5.7 %all-to-all-start = ((bf16[16,416,128]{2,1,0:T(8,128)(2,1)}), bf16[16,416,128]{2,1,0:T(8,128)(2,1)S(1)}, u32[]{:S(2)}, u32[]{:S(2)}) async-start(bf16[16,416,128]{2,1,0:T(8,128)(2,1)} %lookup.1), calls=%async_computation | async-start | bytes 3407872 | tf_op jit(solution)/shard_map/all_to_all | solution.py:279
  34.6 61.0 %collective-permute-done = bf16[1664,1024]{1,0:T(8,128)(2,1)} collective-permute-done((bf16[1664,1024]{1,0:T(8,128)(2,1)}, bf16[1664,1024]{1,0:T(8,128)(2,1)}, u32[]{:S(2)}, u32[]{:S(2)}) %collective-permute-start) | collective-permute-done | bytes 3407904 | tf_op jit(solution)/shard_map/ppermute | solution.py:193
  95.6 1.5 collective-permute-start.1
  97.1 0.5 collective-permute-start.2
  97.6 1.6 collective-permute-done.1
  99.2 1.5 collective-permute-done.2
  100.7 1.3 copy-done
  102.0 22.9 %pool.1 = bf16[256,1664]{1,0:T(8,128)(2,1)} custom-call(s32[1,416]{1,0:T(1,128)} %bitcast.34, bf16[16,416,128]{2,1,0:T(8,128)(2,1)} %copy-done, s32[16,3328]{1,0:T(8,128)} %get-tuple-element.14.lo_ref, f32[16,3328]{1,0:T(8,128)} %get-tuple-element.15.wo_ref), custom_call_target="tpu_custom_call" | custom-call | tf_op jit(solution)/shard_map/pool/pallas_call | solution.py:284
  124.8 5.7 %multiply_reduce_fusion = (f32[256]{0:T(256)S(1)}, f32[256,2048]{1,0:T(8,128)S(1)}) fusion(f32[2048]{0:T(1024)S(1)} %convert_element_type.43, f32[2048]{0:T(1024)S(1)} %convert_element_type.42, bf16[256,1664]{1,0:T(8,128)(2,1)} %pool.1, bf16[1664,2048]{1,0:T(8,128)(2,1)} %param.15), kind=kOutput, calls=%fused_computation.4 | convolution fusion | flops 1748500224 | bytes 9782272 | tf_op jit(solution)/shard_map/dot_general | solution.py:213
  130.6 3.5 %multiply_reduce_fusion.3 = (f32[256]{0:T(256)S(1)}, f32[256,1024]{1,0:T(8,128)S(1)}) fusion(f32[1024]{0:T(1024)S(1)} %get-tuple-element.24, f32[1024]{0:T(1024)S(1)} %get-tuple-element.26, bf16[256,1664]{1,0:T(8,128)(2,1)S(1)} %copy-done.3, bf16[1664,1024]{1,0:T(8,128)(2,1)} %collective-permute-done), kind=kOutput, calls=%fused_computation.17 | convolution fusion | flops 874249984 | bytes 5317632 | tf_op jit(solution)/shard_map/dot_general | solution.py:213
  134.1 3.5 %multiply_reduce_fusion.2 = (f32[256]{0:T(256)S(1)}, f32[256,1024]{1,0:T(8,128)S(1)}) fusion(f32[1024]{0:T(1024)S(1)} %get-tuple-element.25, f32[1024]{0:T(1024)S(1)} %get-tuple-element.27, bf16[256,1664]{1,0:T(8,128)(2,1)S(1)} %copy-done.3, bf16[1664,1024]{1,0:T(8,128)(2,1)} %collective-permute-done.3), kind=kOutput, calls=%fused_computation.15 | convolution fusion | flops 874249984 | bytes 5317632 | tf_op jit(solution)/shard_map/dot_general | solution.py:213
  137.7 2.7 %fusion = f32[256,1664]{1,0:T(8,128)S(1)} fusion(bf16[1664,2048]{1,0:T(8,128)(2,1)S(1)} %bitcast.24, f32[256,2048]{1,0:T(8,128)S(1)} %get-tuple-element.31, f32[256]{0:T(256)S(1)} %divide_subtract_fusion.1, f32[2048]{0:T(1024)S(1)} %convert_element_type.43), kind=kOutput, calls=%fused_computation.8 | convolution fusion | flops 1750073344 | bytes 10626048 | tf_op jit(solution)/shard_map/dot_general | solution.py:222
  140.4 3.5 %convolution_add_fusion.1 = f32[256,1664]{1,0:T(8,128)S(1)} fusion(f32[256,1664]{1,0:T(8,128)S(1)} %fusion, bf16[1664,1024]{1,0:T(8,128)(2,1)} %collective-permute-done, f32[256,1024]{1,0:T(8,128)S(1)} %get-tuple-element.33, f32[256]{0:T(256)S(1)} %divide_subtract_fusion.1, f32[1024]{0:T(1024)S(1)} %get-tuple-element.24), kind=kOutput, calls=%fused_computation.1 | convolution fusion | flops 875462656 | bytes 7869440 | tf_op jit(solution)/shard_map/dot_general | solution.py:222
  143.8 4.7 %convolution_add_fusion.dp_ref = f32[256,1664]{1,0:T(8,128)} fusion(f32[256,1664]{1,0:T(8,128)S(1)} %convolution_add_fusion.1, bf16[1664,1024]{1,0:T(8,128)(2,1)} %collective-permute-done.3, f32[256,1024]{1,0:T(8,128)S(1)} %get-tuple-element.29, f32[256]{0:T(256)S(1)} %divide_subtract_fusion.1, f32[1024]{0:T(1024)S(1)} %get-tuple-element.25), kind=kOutput, calls=%fused_computation | convolution fusion | flops 875462656 | bytes 7869440 | tf_op jit(solution)/shard_map/dot_general | solution.py:222
  148.5 30.3 %backward.1 = (bf16[16,416,128]{2,1,0:T(8,128)(2,1)}, f32[4,3328]{1,0:T(4,128)}) custom-call(s32[416,1]{1,0:T(8,128)} %get-tuple-element.13.uniq_ref, bf16[16,416,128]{2,1,0:T(8,128)(2,1)} %copy-done, s32[16,3328]{1,0:T(8,128)} %get-tuple-element.14.lo_ref, f32[16,3328]{1,0:T(8,128)} %get-tuple-element.15.wo_ref, s32[4,3328]{1,0:T(4,128)} %bitcast.30, ...), custom_call_target="tpu_custom_call" | custom-call | tf_op jit(solution)/shard_map/backward/pallas_call | solution.py:295
  178.8 46.4 %all_to_all.10.got_ref = bf16[16,416,128]{2,1,0:T(8,128)(2,1)} all-to-all(bf16[16,416,128]{2,1,0:T(8,128)(2,1)} %get-tuple-element.17), channel_id=1, replica_groups=mesh['owner'=16,'dense'=2] {'owner'}, dimensions={0} | all-to-all | bytes 3407872 | tf_op jit(solution)/shard_map/all_to_all | solution.py:312
  225.2 5.5 %collect.2 = bf16[1024,128]{1,0:T(8,128)(2,1)} custom-call(s32[16,512]{1,0:T(8,128)} %bitcast.26, bf16[16,416,128]{2,1,0:T(8,128)(2,1)} %all_to_all.10.got_ref), custom_call_target="tpu_custom_call" | custom-call | tf_op jit(solution)/shard_map/collect/pallas_call | solution.py:316
  230.7 0.5 collective-permute-start.4
  231.2 5.5 %collect.3 = bf16[1024,128]{1,0:T(8,128)(2,1)} custom-call(s32[16,512]{1,0:T(8,128)} %bitcast.27, bf16[16,416,128]{2,1,0:T(8,128)(2,1)} %all_to_all.10.got_ref), custom_call_target="tpu_custom_call" | custom-call | tf_op jit(solution)/shard_map/collect/pallas_call | solution.py:316
  236.7 1.5 collective-permute-start.5
  238.2 0.7 copy.13
  238.9 0.4 collective-permute-done.4
  239.4 5.6 %collective-permute-done.5 = bf16[1024,128]{1,0:T(8,128)(2,1)S(1)} collective-permute-done((bf16[1024,128]{1,0:T(8,128)(2,1)}, bf16[1024,128]{1,0:T(8,128)(2,1)S(1)}, u32[]{:S(2)}, u32[]{:S(2)}) %collective-permute-start.5) | collective-permute-done | bytes 262176 | tf_op jit(solution)/shard_map/ppermute | solution.py:328
  245.0 1.0 convert_add_fusion
  246.4 0.6 fusion.13
  247.0 1.3 divide_subtract_fusion
  (33 shorter events, 0.5 us)
Async XLA Ops:
  19.5 76.1 %collective-permute-start = (bf16[1664,1024]{1,0:T(8,128)(2,1)}, bf16[1664,1024]{1,0:T(8,128)(2,1)}, u32[]{:S(2)}, u32[]{:S(2)}) collective-permute-start(bf16[1664,1024]{1,0:T(8,128)(2,1)} %constant_dynamic-slice_fusion), channel_id=1, source_target_pairs={{0,1},{1,0},{2,3},{3,2},{4,5},{5,4},{6,7},{7,6},{8,9},{9,8},{10,11... | collective-permute-start | bytes 10223624 | tf_op jit(solution)/shard_map/ppermute | solution.py:193
  28.9 66.7 %copy-start.6 = (bf16[2048]{0:T(1024)(128)(2,1)S(1)}, bf16[2048]{0:T(1024)(128)(2,1)}, u32[]{:S(2)}) copy-start(bf16[2048]{0:T(1024)(128)(2,1)} %param.16) | copy-start | bytes 12292
  28.9 68.3 %copy-start.7 = (bf16[2048]{0:T(1024)(128)(2,1)S(1)}, bf16[2048]{0:T(1024)(128)(2,1)}, u32[]{:S(2)}) copy-start(bf16[2048]{0:T(1024)(128)(2,1)} %param.17) | copy-start | bytes 12292
  28.9 71.9 %all-to-all-start = ((bf16[16,416,128]{2,1,0:T(8,128)(2,1)}), bf16[16,416,128]{2,1,0:T(8,128)(2,1)S(1)}, u32[]{:S(2)}, u32[]{:S(2)}) async-start(bf16[16,416,128]{2,1,0:T(8,128)(2,1)} %lookup.1), calls=%async_computation | async-start | bytes 3407872 | tf_op jit(solution)/shard_map/all_to_all | solution.py:279
  95.6 38.5 %collective-permute-start.3 = (bf16[1664,1024]{1,0:T(8,128)(2,1)}, bf16[1664,1024]{1,0:T(8,128)(2,1)}, u32[]{:S(2)}, u32[]{:S(2)}) collective-permute-start(bf16[1664,1024]{1,0:T(8,128)(2,1)} %collective-permute-done), channel_id=1, source_target_pairs={{0,2},{2,0},{4,6},{6,4},{8,10},{10,8},{12,14},{14,12},{16,18},{18,... | collective-permute-start | bytes 10223624 | tf_op jit(solution)/shard_map/ppermute | solution.py:196
  95.6 3.6 %collective-permute-start.1 = (bf16[2048]{0:T(1024)(128)(2,1)S(1)}, bf16[2048]{0:T(1024)(128)(2,1)S(1)}, u32[]{:S(2)}, u32[]{:S(2)}) collective-permute-start(bf16[2048]{0:T(1024)(128)(2,1)S(1)} %copy-done.6), channel_id=1, source_target_pairs={{0,1},{1,0},{2,3},{3,2},{4,5},{5,4},{6,7},{7,6},{8,9},{9,8},{10,11... | collective-permute-start | bytes 12296 | tf_op jit(solution)/shard_map/ppermute | solution.py:194
  97.1 3.6 %collective-permute-start.2 = (bf16[2048]{0:T(1024)(128)(2,1)S(1)}, bf16[2048]{0:T(1024)(128)(2,1)S(1)}, u32[]{:S(2)}, u32[]{:S(2)}) collective-permute-start(bf16[2048]{0:T(1024)(128)(2,1)S(1)} %copy-done.7), channel_id=1, source_target_pairs={{0,1},{1,0},{2,3},{3,2},{4,5},{5,4},{6,7},{7,6},{8,9},{9,8},{10,11... | collective-permute-start | bytes 12296 | tf_op jit(solution)/shard_map/ppermute | solution.py:195
  100.7 1.3 copy-start
  124.8 5.7 %copy-start.3 = (bf16[256,1664]{1,0:T(8,128)(2,1)S(1)}, bf16[256,1664]{1,0:T(8,128)(2,1)}, u32[]{:S(2)}) copy-start(bf16[256,1664]{1,0:T(8,128)(2,1)} %pool.1) | copy-start | bytes 2555908
  130.6 7.1 %slice-start = ((s8[6815744]{0:T(1024)(128)(4,1)}), s8[4194304]{0:T(1024)(128)(4,1)S(1)}, s32[]{:S(2)}) async-start(s8[6815744]{0:T(1024)(128)(4,1)} %bitcast.23), calls=%async_computation.2 | async-start | bytes 8388608
  134.1 3.5 %copy-start.8 = (bf16[256]{0:T(256)(128)(2,1)S(1)}, bf16[256]{0:T(256)(128)(2,1)}, u32[]{:S(2)}) copy-start(bf16[256]{0:T(256)(128)(2,1)} %param.12) | copy-start | bytes 1540
  134.1 3.6 %slice-start.1 = ((s8[6815744]{0:T(1024)(128)(4,1)}), s8[2621440]{0:T(1024)(128)(4,1)S(1)}, s32[]{:S(2)}) async-start(s8[6815744]{0:T(1024)(128)(4,1)} %bitcast.23), calls=%async_computation.3 | async-start | bytes 5242880
  225.2 13.0 %copy-start.4 = (f32[4,3328]{1,0:T(4,128)S(1)}, f32[4,3328]{1,0:T(4,128)}, u32[]{:S(2)}) copy-start(f32[4,3328]{1,0:T(4,128)} %get-tuple-element.18) | copy-start | bytes 159748
  230.7 8.6 %copy-start.2 = (bf16[1024,128]{1,0:T(8,128)(2,1)S(1)}, bf16[1024,128]{1,0:T(8,128)(2,1)}, u32[]{:S(2)}) copy-start(bf16[1024,128]{1,0:T(8,128)(2,1)} %collect.2) | copy-start | bytes 786436
  230.7 8.6 %collective-permute-start.4 = (bf16[1024,128]{1,0:T(8,128)(2,1)}, bf16[1024,128]{1,0:T(8,128)(2,1)S(1)}, u32[]{:S(2)}, u32[]{:S(2)}) collective-permute-start(bf16[1024,128]{1,0:T(8,128)(2,1)} %collect.2), channel_id=1, source_target_pairs={{0,1},{1,0},{2,3},{3,2},{4,5},{5,4},{6,7},{7,6},{8,9},{9,8},{10,11... | collective-permute-start | bytes 786440 | tf_op jit(solution)/shard_map/ppermute | solution.py:328
  236.7 9.7 %copy-start.5 = (f32[2048]{0:T(1024)S(1)}, f32[2048]{0:T(1024)}, u32[]{:S(2)}) copy-start(f32[2048]{0:T(1024)} %param.14) | copy-start | bytes 24580
  236.7 10.3 %copy-start.1 = (f32[2048,128]{1,0:T(8,128)S(1)}, f32[2048,128]{1,0:T(8,128)}, u32[]{:S(2)}) copy-start(f32[2048,128]{1,0:T(8,128)} %table_ref.1) | copy-start | bytes 3145732
  236.7 8.4 %collective-permute-start.5 = (bf16[1024,128]{1,0:T(8,128)(2,1)}, bf16[1024,128]{1,0:T(8,128)(2,1)S(1)}, u32[]{:S(2)}, u32[]{:S(2)}) collective-permute-start(bf16[1024,128]{1,0:T(8,128)(2,1)} %collect.3), channel_id=1, source_target_pairs={{0,1},{1,0},{2,3},{3,2},{4,5},{5,4},{6,7},{7,6},{8,9},{9,8},{10,11... | collective-permute-start | bytes 786440 | tf_op jit(solution)/shard_map/ppermute | solution.py:328

commit v3 on v2

--- a/solution.py
+++ b/solution.py
@@ -124,15 +124,16 @@
 
 
 def backward_body(
-    uniq_ref, rows_ref, lo_ref, wo_ref, own_ref, w_ref, dp_ref, grad_ref, wg_ref, acc, wide
+    start, last, uniq_ref, rows_ref, lo_ref, wo_ref, own_ref, w_ref, dp_ref, before_ref,
+    grad_ref, wg_ref, acc, wide
 ):
-    groups = rows_ref.shape[0]
+    groups, uniq, _ = grad_ref.shape
     f = pl.program_id(0)
 
     @pl.when(f == 0)
     def _():
         acc[...] = jnp.zeros_like(acc)
-        wide[...] = jnp.broadcast_to(uniq_ref[...], wide.shape)
+        wide[...] = jnp.broadcast_to(uniq_ref[start : start + uniq, :], wide.shape)
 
     dp = dp_ref[...]
     dp_rows = dp.astype(bf16)
@@ -141,58 +142,70 @@
     own = own_ref[...]
     total = jnp.sum(slot_w, axis=0, keepdims=True)
     scaled = wo_ref[...] / total
-    along = jnp.zeros(slot_w.shape, f32)
+    along = before_ref[...]
     for o in range(groups):
         hit = wide[...] == lo_ref[o : o + 1, :]
         mix = jnp.where(hit, scaled[o : o + 1, :], 0.0).astype(bf16)
         acc[o] += jnp.dot(mix, dp_rows, preferred_element_type=f32)
-        dots = jnp.dot(rows_ref[o], dp_cols, preferred_element_type=f32)
+        rows = rows_ref[o, start : start + uniq, :]
+        dots = jnp.dot(rows, dp_cols, preferred_element_type=f32)
         mine = jnp.sum(jnp.where(hit, dots, 0.0), axis=0, keepdims=True)
         along += jnp.where(own == o, mine, 0.0)
-    centre = jnp.sum(slot_w * along, axis=0, keepdims=True) / total
-    wg_ref[...] = (along - centre) / total
+    if last:
+        centre = jnp.sum(slot_w * along, axis=0, keepdims=True) / total
+        wg_ref[...] = (along - centre) / total
+    else:
+        wg_ref[...] = along
 
     @pl.when(f == pl.num_programs(0) - 1)
     def _():
         grad_ref[...] = acc[...].astype(bf16)
 
 
-def collect_body(base, list_ref, got_ref, out_ref, columns, acc):
-    groups, uniq, width = got_ref.shape
+def collect_body(base, list_ref, *refs):
+    *got_refs, out_ref, columns, acc = refs
+    groups, _, width = got_refs[0].shape
     half = out_ref.shape[0] // 2
     columns[...] = list_ref[...].T - base
-    at = lax.broadcasted_iota(jnp.int32, (half, uniq), 0)
-    for q in range(groups):
-        row = list_ref[q : q + 1, :uniq] - base
-        row = jnp.where(row >= half, row - half, row)
-        pick = jnp.where(row == at, 1.0, 0.0).astype(bf16)
-        ids = columns[:uniq, q : q + 1]
-        got = got_ref[q].astype(f32)
-        first = jnp.where(ids < half, got, 0.0)
-        second = jnp.where(ids >= half, got, 0.0)
-        both = jnp.concatenate([first, second], axis=1).astype(bf16)
-        term = jnp.dot(pick, both, preferred_element_type=f32)
-        if q == 0:
-            acc[...] = term
-        else:
-            acc[...] += term
+    acc[...] = jnp.zeros_like(acc)
+    start = 0
+    for got_ref in got_refs:
+        uniq = got_ref.shape[1]
+        at = lax.broadcasted_iota(jnp.int32, (half, uniq), 0)
+        for q in range(groups):
+            row = list_ref[q : q + 1, start : start + uniq] - base
+            row = jnp.where(row >= half, row - half, row)
+            pick = jnp.where(row == at, 1.0, 0.0).astype(bf16)
+            ids = columns[start : start + uniq, q : q + 1]
+            got = got_ref[q].astype(f32)
+            first = jnp.where(ids < half, got, 0.0)
+            second = jnp.where(ids >= half, got, 0.0)
+            both = jnp.concatenate([first, second], axis=1).astype(bf16)
+            acc[...] += jnp.dot(pick, both, preferred_element_type=f32)
+        start += uniq
     out_ref[:half] = acc[:, :width].astype(bf16)
     out_ref[half:] = acc[:, width:].astype(bf16)
 
 
-def head_pieces(w_in, b_in, w_out):
-    groups = lax.axis_size("owner")
+def send_weights(w_in, b_in, w_out):
     parts = lax.axis_size("dense")
     half = w_in.shape[1] // 2
     core = lax.rem(lax.axis_index("owner"), 2)
-    pieces = [(w_in, b_in, w_out)]
     mine = lax.dynamic_slice_in_dim(w_in, core * half, half, axis=1)
-    swap = [(g, g + 1 - 2 * (g % 2)) for g in range(groups)]
+    arrived = []
     for shift in range(1, parts):
         ring = [(d, (d + shift) % parts) for d in range(parts)]
-        w_here = lax.ppermute(mine, "dense", ring)
-        b_all = lax.ppermute(b_in, "dense", ring)
-        o_all = lax.ppermute(w_out, "dense", ring)
+        arrived.append(tuple(lax.ppermute(x, "dense", ring) for x in (mine, b_in, w_out)))
+    return arrived
+
+
+def head_pieces(w_in, b_in, w_out, arrived):
+    groups = lax.axis_size("owner")
+    half = w_in.shape[1] // 2
+    core = lax.rem(lax.axis_index("owner"), 2)
+    swap = [(g, g + 1 - 2 * (g % 2)) for g in range(groups)]
+    pieces = [(w_in, b_in, w_out)]
+    for w_here, b_all, o_all in arrived:
         w_there = lax.ppermute(w_here, "owner", swap)
         for w_piece, at in ((w_here, core * half), (w_there, (1 - core) * half)):
             pieces.append(
@@ -232,6 +245,7 @@
     bags = samples * fields
     uniq = bags * bag_len // (2 * groups)
     padded = -(-uniq // lane) * lane
+    arrived = send_weights(w_in, b_in, w_out)
 
     def by_slot(x):
         return x.transpose(2, 1, 0).reshape(bag_len, bags)
@@ -262,8 +276,6 @@
         compiler_params=pltpu.CompilerParams(collective_id=0, has_side_effects=True),
         name="share",
     )(distinct_row).reshape(groups, padded)
-    lists, w_later = lax.optimization_barrier((lists, w_in))
-    pieces = head_pieces(w_later, b_in, w_out)
     depth = table_rows // 4
     found = pl.pallas_call(
         lookup_body,
@@ -290,40 +302,52 @@
         name="pool",
     )(distinct_row[:, :uniq], rows, named, spread)
 
+    inputs, arrived = lax.optimization_barrier((inputs, arrived))
+    pieces = head_pieces(w_in, b_in, w_out, arrived)
     dinputs = head(inputs, labels, pieces)
 
-    grads, weight_grad = pl.pallas_call(
-        backward_body,
-        grid=(fields,),
-        out_shape=(
-            jax.ShapeDtypeStruct((groups, uniq, width), bf16),
-            jax.ShapeDtypeStruct((bag_len, bags), f32),
-        ),
-        in_specs=[vmem(), vmem(), block, block, slots, slots, field],
-        out_specs=(vmem(), slots),
-        scratch_shapes=[
-            pltpu.VMEM((groups, uniq, width), f32),
-            pltpu.VMEM((uniq, samples), jnp.int32),
-        ],
-        name="backward",
-    )(distinct, rows, named, spread, own, w, dinputs)
+    spans = [(0, uniq)]
+    weight_grad = jnp.zeros((bag_len, bags), f32)
+    got = []
+    for start, count in spans:
+        last = start + count == uniq
+        grads, weight_grad = pl.pallas_call(
+            functools.partial(backward_body, start, last),
+            grid=(fields,),
+            out_shape=(
+                jax.ShapeDtypeStruct((groups, count, width), bf16),
+                jax.ShapeDtypeStruct((bag_len, bags), f32),
+            ),
+            in_specs=[vmem(), vmem(), block, block, slots, slots, field, slots],
+            out_specs=(vmem(), slots),
+            scratch_shapes=[
+                pltpu.VMEM((groups, count, width), f32),
+                pltpu.VMEM((count, samples), jnp.int32),
+            ],
+            name="backward",
+            cost_estimate=pl.CostEstimate(
+                flops=4 * groups * count * width * bags,
+                bytes_accessed=4 * groups * count * width,
+                transcendentals=0,
+            ),
+        )(distinct, rows, named, spread, own, w, dinputs, weight_grad)
+        got.append(lax.all_to_all(grads, "owner", split_axis=0, concat_axis=0, tiled=True))
     weight_grad = weight_grad.reshape(bag_len, fields, samples).transpose(2, 1, 0)
 
-    got = lax.all_to_all(grads, "owner", split_axis=0, concat_axis=0, tiled=True)
     chunk = table_rows // 2
     sums = []
     for base in range(0, table_rows, chunk):
         row_part = pl.pallas_call(
             functools.partial(collect_body, base),
             out_shape=jax.ShapeDtypeStruct((chunk, width), bf16),
-            in_specs=[vmem(), vmem()],
+            in_specs=[vmem()] * (1 + len(got)),
             out_specs=vmem(),
             scratch_shapes=[
                 pltpu.VMEM((padded, groups), jnp.int32),
                 pltpu.VMEM((chunk // 2, 2 * width), f32),
             ],
             name="collect",
-        )(lists, got)
+        )(lists, *got)
         if parts == 2:
             other = lax.ppermute(row_part, "dense", [(0, 1), (1, 0)])
             sums.append(row_part.astype(f32) + other.astype(f32))

time: 249 us -> 222 us (0.89)
  waiting for transfers between devices: 70.2 us -> 38.1 us
  blocking collectives: 46.4 us -> 49.9 us
  starting transfers between devices: 11.3 us -> 13.8 us
    ppermute x3, waiting for transfers between devices: 64.1 us -> 0.01 us  [send_weights(): lax.ppermute(x, 'dense', ring)]
    all_to_all x1, waiting for transfers between devices: 0.01 us -> 32 us  [local(): lax.all_to_all(found, 'owner', split_axis=0, concat_axis=0, tiled=True)]
    all_to_all x1, blocking collectives: 46.4 us -> 49.9 us  [local(): lax.all_to_all(grads, 'owner', split_axis=0, concat_axis=0, tiled=True)]
  transfers between devices with their start and end apart: 7 -> 7, of which waited for: 5 -> 3; matrix products, arithmetic and copies ran while one was open for 4% -> 5% of each run, Pallas kernels for 15% -> 22%
where the time goes in v3:
time: 222 us
  Pallas kernels  84 us (38%)
  blocking collectives  49.9 us (22%)
  waiting for transfers between devices  38.1 us (17%)
  matrix products  23.5 us (11%)
  starting transfers between devices  13.8 us (6%)
  local copies, waits for them, and re-layouts  8.05 us (4%)
  other arithmetic  3.34 us (2%)
    all_to_all x1, blocking collectives, local(): lax.all_to_all(grads, 'owner', split_axis=0, concat_axis=0, tiled=True)  49.9 us
    all_to_all x1, waiting for transfers between devices, local(): lax.all_to_all(found, 'owner', split_axis=0, concat_axis=0, tiled=True)  32 us
    pallas_call x1, Pallas kernels, local(): pl.pallas_call(functools.partial(backward_body, start, last), grid=(field...  30.4 us
    pallas_call x1, Pallas kernels, local(): pl.pallas_call(pool_body, grid=(fields,), out_shape=jax.ShapeDtypeStruct(...  22.9 us
    dot_general x3, matrix products, head(): preact = jnp.dot(inputs, w, preferred_element_type=f32) + b.astype(f32)  12.7 us
    pallas_call x2, Pallas kernels, local(): pl.pallas_call(functools.partial(collect_body, base), out_shape=jax.Shape...  11 us
    dot_general x3, matrix products, head(): lax.dot_general(dhidden, w, (((1,), (1,)), ((), ())), preferred_element_t...  10.8 us
    pallas_call x1, Pallas kernels, local(): pl.pallas_call(functools.partial(share_body, groups), out_shape=jax.Shape...  8.44 us
  transfers between devices with their start and end apart: 7, of which 3 were waited for; matrix products, arithmetic and copies ran while one was open for 5% of the time, Pallas kernels for 22%

profile of v3, /device:TPU:0, one launch (start us, length us, event | category | flops | bytes accessed | tf_op | source)
XLA Modules:
  0.0 221.6 jit_solution(220244141539371413)
XLA Ops:
  0.6 4.1 %constant_dynamic-slice_fusion = bf16[1664,1024]{1,0:T(8,128)(2,1)} fusion(bf16[1664,2048]{1,0:T(8,128)(2,1)} %param.15, s32[]{:T(128)S(6)} %select_n.4), kind=kLoop, calls=%fused_computation.36 | loop fusion | bytes 6815748 | tf_op jit(solution)/shard_map/dynamic_slice | solution.py:194
  4.7 3.0 %collective-permute-start = (bf16[1664,1024]{1,0:T(8,128)(2,1)}, bf16[1664,1024]{1,0:T(8,128)(2,1)}, u32[]{:S(2)}, u32[]{:S(2)}) collective-permute-start(bf16[1664,1024]{1,0:T(8,128)(2,1)} %constant_dynamic-slice_fusion), channel_id=1, source_target_pairs={{0,1},{1,0},{2,3},{3,2},{4,5},{5,4},{6,7},{7,6},{8,9},{9,8},{10,11... | collective-permute-start | bytes 10223624 | tf_op jit(solution)/shard_map/ppermute | solution.py:198
  7.7 3.5 %distinct.1 = (s32[416,1]{1,0:T(8,128)}, s32[1,512]{1,0:T(1,128)}, s32[16,3328]{1,0:T(8,128)}, f32[16,3328]{1,0:T(8,128)}) custom-call(s32[4,3328]{1,0:T(4,128)} %bitcast.30, s32[4,3328]{1,0:T(4,128)} %bitcast.29, f32[4,3328]{1,0:T(4,128)} %bitcast.32), custom_call_target="tpu_custom_call" | custom-call | tf_op jit(solution)/shard_map/distinct/pallas_call | solution.py:254
  11.2 8.4 %share.1 = s32[16,1,512]{2,1,0:T(1,128)} custom-call(s32[1,512]{1,0:T(1,128)} %get-tuple-element.13.row_ref), custom_call_target="tpu_custom_call" | custom-call | tf_op jit(solution)/shard_map/share/pallas_call | solution.py:266
  19.7 1.4 copy.16
  21.0 7.8 %lookup.1 = bf16[16,416,128]{2,1,0:T(8,128)(2,1)} custom-call(s32[16,512]{1,0:T(8,128)} %bitcast.25, f32[2048,128]{1,0:T(8,128)} %table_ref.1), custom_call_target="tpu_custom_call" | custom-call | tf_op jit(solution)/shard_map/lookup/pallas_call | solution.py:280
  28.8 5.7 %all-to-all-start = ((bf16[16,416,128]{2,1,0:T(8,128)(2,1)}), bf16[16,416,128]{2,1,0:T(8,128)(2,1)S(1)}, u32[]{:S(2)}, u32[]{:S(2)}) async-start(bf16[16,416,128]{2,1,0:T(8,128)(2,1)} %lookup.1), calls=%async_computation | async-start | bytes 3407872 | tf_op jit(solution)/shard_map/all_to_all | solution.py:291
  34.6 0.6 collective-permute-start.1
  35.1 1.5 collective-permute-start.2
  36.7 32.0 %all-to-all-done.rows_ref = bf16[16,416,128]{2,1,0:T(8,128)(2,1)S(1)} async-done(((bf16[16,416,128]{2,1,0:T(8,128)(2,1)}), bf16[16,416,128]{2,1,0:T(8,128)(2,1)S(1)}, u32[]{:S(2)}, u32[]{:S(2)}) %all-to-all-start) | async-done | bytes 1703968 | tf_op jit(solution)/shard_map/all_to_all | solution.py:291
  68.7 1.3 copy-done
  69.9 22.9 %pool.1 = bf16[256,1664]{1,0:T(8,128)(2,1)} custom-call(s32[1,416]{1,0:T(1,128)} %bitcast.34, bf16[16,416,128]{2,1,0:T(8,128)(2,1)} %copy-done, s32[16,3328]{1,0:T(8,128)} %get-tuple-element.15.lo_ref, f32[16,3328]{1,0:T(8,128)} %get-tuple-element.16.wo_ref), custom_call_target="tpu_custom_call" | custom-call | tf_op jit(solution)/shard_map/pool/pallas_call | solution.py:296
  92.8 1.0 collective-permute-start.3
  93.9 3.7 %multiply_reduce_fusion.3 = (f32[256]{0:T(256)S(1)}, f32[256,1024]{1,0:T(8,128)S(1)}) fusion(f32[1024]{0:T(1024)S(1)} %get-tuple-element.28, f32[1024]{0:T(1024)S(1)} %get-tuple-element.39, bf16[256,1664]{1,0:T(8,128)(2,1)} %pool.1, bf16[1664,1024]{1,0:T(8,128)(2,1)} %collective-permute-done), kind=kOutput, calls=%fused_computation.17 | convolution fusion | flops 874249984 | bytes 5317632 | tf_op jit(solution)/shard_map/dot_general | solution.py:226
  97.6 5.6 %multiply_reduce_fusion = (f32[256]{0:T(256)S(1)}, f32[256,2048]{1,0:T(8,128)S(1)}) fusion(f32[2048]{0:T(1024)S(1)} %convert_element_type.43, f32[2048]{0:T(1024)S(1)} %convert_element_type.42, bf16[256,1664]{1,0:T(8,128)(2,1)S(1)} %copy-done.3, bf16[1664,2048]{1,0:T(8,128)(2,1)} %param.15), kind=kOutput, calls=%fused_computation.4 | convolution fusion | flops 1748500224 | bytes 9782272 | tf_op jit(solution)/shard_map/dot_general | solution.py:226
  103.2 3.4 %multiply_reduce_fusion.2 = (f32[256]{0:T(256)S(1)}, f32[256,1024]{1,0:T(8,128)S(1)}) fusion(f32[1024]{0:T(1024)S(1)} %get-tuple-element.29, f32[1024]{0:T(1024)S(1)} %get-tuple-element.38, bf16[256,1664]{1,0:T(8,128)(2,1)S(1)} %copy-done.3, bf16[1664,1024]{1,0:T(8,128)(2,1)} %collective-permute-done.3), kind=kOutput, calls=%fused_computation.15 | convolution fusion | flops 874249984 | bytes 5317632 | tf_op jit(solution)/shard_map/dot_general | solution.py:226
  106.7 2.7 %fusion = f32[256,1664]{1,0:T(8,128)S(1)} fusion(bf16[1664,2048]{1,0:T(8,128)(2,1)S(1)} %bitcast.24, f32[256,2048]{1,0:T(8,128)S(1)} %get-tuple-element.35, f32[256]{0:T(256)S(1)} %divide_subtract_fusion.1, f32[2048]{0:T(1024)S(1)} %convert_element_type.43), kind=kOutput, calls=%fused_computation.8 | convolution fusion | flops 1750073344 | bytes 10626048 | tf_op jit(solution)/shard_map/dot_general | solution.py:235
  109.3 3.4 %convolution_add_fusion.1 = f32[256,1664]{1,0:T(8,128)S(1)} fusion(f32[256,1664]{1,0:T(8,128)S(1)} %fusion, bf16[1664,1024]{1,0:T(8,128)(2,1)} %collective-permute-done, f32[256,1024]{1,0:T(8,128)S(1)} %get-tuple-element.37, f32[256]{0:T(256)S(1)} %divide_subtract_fusion.1, f32[1024]{0:T(1024)S(1)} %get-tuple-element.28), kind=kOutput, calls=%fused_computation.1 | convolution fusion | flops 875462656 | bytes 7869440 | tf_op jit(solution)/shard_map/dot_general | solution.py:235
  112.8 4.7 %convolution_add_fusion.dp_ref = f32[256,1664]{1,0:T(8,128)} fusion(f32[256,1664]{1,0:T(8,128)S(1)} %convolution_add_fusion.1, bf16[1664,1024]{1,0:T(8,128)(2,1)} %collective-permute-done.3, f32[256,1024]{1,0:T(8,128)S(1)} %get-tuple-element.33, f32[256]{0:T(256)S(1)} %divide_subtract_fusion.1, f32[1024]{0:T(1024)S(1)} %get-tuple-element.29), kind=kOutput, calls=%fused_computation | convolution fusion | flops 875462656 | bytes 7869440 | tf_op jit(solution)/shard_map/dot_general | solution.py:235
  117.4 0.6 broadcast_in_dim.2.before_ref
  118.1 30.4 %backward.1 = (bf16[16,416,128]{2,1,0:T(8,128)(2,1)}, f32[4,3328]{1,0:T(4,128)}) custom-call(s32[416,1]{1,0:T(8,128)} %get-tuple-element.14.uniq_ref, bf16[16,416,128]{2,1,0:T(8,128)(2,1)} %copy-done, s32[16,3328]{1,0:T(8,128)} %get-tuple-element.15.lo_ref, f32[16,3328]{1,0:T(8,128)} %get-tuple-element.16.wo_ref, s32[4,3328]{1,0:T(4,128)} %bitcast.31, ...), custom_call_target="tpu_custom_call" | custom-call | flops 11341398016 | bytes 3407872 | tf_op jit(solution)/shard_map/backward/pallas_call | solution.py:314
  148.5 49.9 %all_to_all.10.refs_0_ = bf16[16,416,128]{2,1,0:T(8,128)(2,1)} all-to-all(bf16[16,416,128]{2,1,0:T(8,128)(2,1)} %get-tuple-element.21), channel_id=1, replica_groups=mesh['owner'=16,'dense'=2] {'owner'}, dimensions={0} | all-to-all | bytes 3407872 | tf_op jit(solution)/shard_map/all_to_all | solution.py:334
  198.4 5.5 %collect.3 = bf16[1024,128]{1,0:T(8,128)(2,1)} custom-call(s32[16,512]{1,0:T(8,128)} %bitcast.26, bf16[16,416,128]{2,1,0:T(8,128)(2,1)} %all_to_all.10.refs_0_), custom_call_target="tpu_custom_call" | custom-call | tf_op jit(solution)/shard_map/collect/pallas_call | solution.py:340
  203.9 0.5 collective-permute-start.5
  204.4 5.5 %collect.2 = bf16[1024,128]{1,0:T(8,128)(2,1)} custom-call(s32[16,512]{1,0:T(8,128)} %bitcast.27, bf16[16,416,128]{2,1,0:T(8,128)(2,1)} %all_to_all.10.refs_0_), custom_call_target="tpu_custom_call" | custom-call | tf_op jit(solution)/shard_map/collect/pallas_call | solution.py:340
  209.9 1.5 collective-permute-start.4
  211.5 0.7 copy.13
  212.1 0.4 collective-permute-done.5
  212.6 5.7 %collective-permute-done.4 = bf16[1024,128]{1,0:T(8,128)(2,1)S(1)} collective-permute-done((bf16[1024,128]{1,0:T(8,128)(2,1)}, bf16[1024,128]{1,0:T(8,128)(2,1)S(1)}, u32[]{:S(2)}, u32[]{:S(2)}) %collective-permute-start.4) | collective-permute-done | bytes 262176 | tf_op jit(solution)/shard_map/ppermute | solution.py:352
  218.3 1.0 convert_add_fusion.1
  219.6 0.6 fusion.13
  220.2 1.3 divide_subtract_fusion
  (33 shorter events, 0.5 us)
Async XLA Ops:
  4.7 88.1 %collective-permute-start = (bf16[1664,1024]{1,0:T(8,128)(2,1)}, bf16[1664,1024]{1,0:T(8,128)(2,1)}, u32[]{:S(2)}, u32[]{:S(2)}) collective-permute-start(bf16[1664,1024]{1,0:T(8,128)(2,1)} %constant_dynamic-slice_fusion), channel_id=1, source_target_pairs={{0,1},{1,0},{2,3},{3,2},{4,5},{5,4},{6,7},{7,6},{8,9},{9,8},{10,11... | collective-permute-start | bytes 10223624 | tf_op jit(solution)/shard_map/ppermute | solution.py:198
  28.8 5.7 %copy-start.7 = (bf16[2048]{0:T(1024)(128)(2,1)S(1)}, bf16[2048]{0:T(1024)(128)(2,1)}, u32[]{:S(2)}) copy-start(bf16[2048]{0:T(1024)(128)(2,1)} %param.16) | copy-start | bytes 12292
  28.8 6.3 %copy-start.6 = (bf16[2048]{0:T(1024)(128)(2,1)S(1)}, bf16[2048]{0:T(1024)(128)(2,1)}, u32[]{:S(2)}) copy-start(bf16[2048]{0:T(1024)(128)(2,1)} %param.17) | copy-start | bytes 12292
  28.8 39.8 %all-to-all-start = ((bf16[16,416,128]{2,1,0:T(8,128)(2,1)}), bf16[16,416,128]{2,1,0:T(8,128)(2,1)S(1)}, u32[]{:S(2)}, u32[]{:S(2)}) async-start(bf16[16,416,128]{2,1,0:T(8,128)(2,1)} %lookup.1), calls=%async_computation | async-start | bytes 3407872 | tf_op jit(solution)/shard_map/all_to_all | solution.py:291
  34.6 58.2 %collective-permute-start.1 = (bf16[2048]{0:T(1024)(128)(2,1)S(1)}, bf16[2048]{0:T(1024)(128)(2,1)S(1)}, u32[]{:S(2)}, u32[]{:S(2)}) collective-permute-start(bf16[2048]{0:T(1024)(128)(2,1)S(1)} %copy-done.7), channel_id=1, source_target_pairs={{0,1},{1,0},{2,3},{3,2},{4,5},{5,4},{6,7},{7,6},{8,9},{9,8},{10,11... | collective-permute-start | bytes 12296 | tf_op jit(solution)/shard_map/ppermute | solution.py:198
  35.1 57.6 %collective-permute-start.2 = (bf16[2048]{0:T(1024)(128)(2,1)S(1)}, bf16[2048]{0:T(1024)(128)(2,1)S(1)}, u32[]{:S(2)}, u32[]{:S(2)}) collective-permute-start(bf16[2048]{0:T(1024)(128)(2,1)S(1)} %copy-done.6), channel_id=1, source_target_pairs={{0,1},{1,0},{2,3},{3,2},{4,5},{5,4},{6,7},{7,6},{8,9},{9,8},{10,11... | collective-permute-start | bytes 12296 | tf_op jit(solution)/shard_map/ppermute | solution.py:198
  68.7 1.3 copy-start
  92.8 10.4 %collective-permute-start.3 = (bf16[1664,1024]{1,0:T(8,128)(2,1)}, bf16[1664,1024]{1,0:T(8,128)(2,1)}, u32[]{:S(2)}, u32[]{:S(2)}) collective-permute-start(bf16[1664,1024]{1,0:T(8,128)(2,1)} %collective-permute-done), channel_id=1, source_target_pairs={{0,2},{2,0},{4,6},{6,4},{8,10},{10,8},{12,14},{14,12},{16,18},{18,... | collective-permute-start | bytes 10223624 | tf_op jit(solution)/shard_map/ppermute | solution.py:209
  93.8 3.7 %copy-start.3 = (bf16[256,1664]{1,0:T(8,128)(2,1)S(1)}, bf16[256,1664]{1,0:T(8,128)(2,1)}, u32[]{:S(2)}) copy-start(bf16[256,1664]{1,0:T(8,128)(2,1)} %pool.1) | copy-start | bytes 2555908
  93.8 12.8 %slice-start = ((s8[6815744]{0:T(1024)(128)(4,1)}), s8[4194304]{0:T(1024)(128)(4,1)S(1)}, s32[]{:S(2)}) async-start(s8[6815744]{0:T(1024)(128)(4,1)} %bitcast.23), calls=%async_computation.2 | async-start | bytes 8388608
  97.6 9.0 %slice-start.1 = ((s8[6815744]{0:T(1024)(128)(4,1)}), s8[2621440]{0:T(1024)(128)(4,1)S(1)}, s32[]{:S(2)}) async-start(s8[6815744]{0:T(1024)(128)(4,1)} %bitcast.23), calls=%async_computation.3 | async-start | bytes 5242880
  103.2 3.4 %copy-start.8 = (bf16[256]{0:T(256)(128)(2,1)S(1)}, bf16[256]{0:T(256)(128)(2,1)}, u32[]{:S(2)}) copy-start(bf16[256]{0:T(256)(128)(2,1)} %param.12) | copy-start | bytes 1540
  198.4 13.0 %copy-start.4 = (f32[4,3328]{1,0:T(4,128)S(1)}, f32[4,3328]{1,0:T(4,128)}, u32[]{:S(2)}) copy-start(f32[4,3328]{1,0:T(4,128)} %get-tuple-element.22) | copy-start | bytes 159748
  203.9 8.6 %copy-start.2 = (bf16[1024,128]{1,0:T(8,128)(2,1)S(1)}, bf16[1024,128]{1,0:T(8,128)(2,1)}, u32[]{:S(2)}) copy-start(bf16[1024,128]{1,0:T(8,128)(2,1)} %collect.3) | copy-start | bytes 786436
  203.9 8.6 %collective-permute-start.5 = (bf16[1024,128]{1,0:T(8,128)(2,1)}, bf16[1024,128]{1,0:T(8,128)(2,1)S(1)}, u32[]{:S(2)}, u32[]{:S(2)}) collective-permute-start(bf16[1024,128]{1,0:T(8,128)(2,1)} %collect.3), channel_id=1, source_target_pairs={{0,1},{1,0},{2,3},{3,2},{4,5},{5,4},{6,7},{7,6},{8,9},{9,8},{10,11... | collective-permute-start | bytes 786440 | tf_op jit(solution)/shard_map/ppermute | solution.py:352
  209.9 9.7 %copy-start.5 = (f32[2048]{0:T(1024)S(1)}, f32[2048]{0:T(1024)}, u32[]{:S(2)}) copy-start(f32[2048]{0:T(1024)} %param.14) | copy-start | bytes 24580
  209.9 10.3 %copy-start.1 = (f32[2048,128]{1,0:T(8,128)S(1)}, f32[2048,128]{1,0:T(8,128)}, u32[]{:S(2)}) copy-start(f32[2048,128]{1,0:T(8,128)} %table_ref.1) | copy-start | bytes 3145732
  209.9 8.4 %collective-permute-start.4 = (bf16[1024,128]{1,0:T(8,128)(2,1)}, bf16[1024,128]{1,0:T(8,128)(2,1)S(1)}, u32[]{:S(2)}, u32[]{:S(2)}) collective-permute-start(bf16[1024,128]{1,0:T(8,128)(2,1)} %collect.2), channel_id=1, source_target_pairs={{0,1},{1,0},{2,3},{3,2},{4,5},{5,4},{6,7},{7,6},{8,9},{9,8},{10,11... | collective-permute-start | bytes 786440 | tf_op jit(solution)/shard_map/ppermute | solution.py:352
